TPU v7x, 768 devices: a whole 4x8x12 slice. The times are simulated.
768 devices in a mesh: dom: 16 (over y, core), event: 48 (over x, z).
Axes of the slice: x: 4, y: 8, z: 12, core: 2. Of those that a mesh axis runs over, the one named last changes fastest.
Arguments:
- adjoint_state: float32 [48, 9, 64, 12288], P('event', None, None, 'dom'), may hold values from -6 to 6
- forward_velocity: float32 [48, 3, 3, 64, 12288], P('event', None, None, None, 'dom'), may hold values from -6 to 6
- density: float32 [64, 12288], P(None, 'dom'), may hold values from 1 to 3
- lame_lambda: float32 [64, 12288], P(None, 'dom'), may hold values from 0.5 to 2
- shear_modulus: float32 [64, 12288], P(None, 'dom'), may hold values from 0.5 to 2
- neighbour: int32 [6, 12288], P(None, 'dom'), may hold values from -1 to 1647, as said below
- send_list: int32 [2, 7040], P(None, 'dom'), may hold values from -1 to 4607, as said below
Outputs:
- adjoint_velocity: float32 [48, 3, 64, 12288], P('event', None, None, 'dom')
- kernels: float32 [3, 16, 49152], P(None, 'dom', 'event')
Inputs may be any that keep to these rules, and one draw needn't show every extreme that they name: `neighbour`: codes 0 to 767 name a slot of the same block, and then that slot's face f xor 1 names this face back; a code 768 + j names position j of row 1 of block b - 1 in send_list, a code 768 + 440 + j position j of row 0 of block b + 1, and such a position holds the partner face; -1 marks outer faces and every face of an unused slot. Every used slot has at least one face with a code other than -1; the used slots of a block come first. In every draw some block uses all 768 slots. `send_list`: positions b * 440 to (b + 1) * 440 - 1 belong to block b: row 0 lists the faces of b whose partner lies in block b - 1, row 1 those whose partner lies in block b + 1, each as f * 768 + s, used positions first and -1 after them. In every draw some block fills all 440 positions of row 0 and some block all 440 of row 1.
All inputs are finite; a program needn't handle non-finite values.
Results may differ from a plain program's by a relative error of at most 0.0001.
Values sent between devices are 32-bit elements; how exact they have to be, the bound alone decides.
A program may use at most 128 MiB of HBM per device.

v0:
```python
import math

import jax
import jax.numpy as jnp
import numpy as np
from jax import lax
from jax.sharding import PartitionSpec as P

time_step = 0.02
lift_weight = 6.0
component_pairs = ((0, 0), (1, 1), (2, 2), (0, 1), (0, 2), (1, 2))
symmetric_index = ((0, 3, 4), (3, 1, 5), (4, 5, 2))


def with_halo(block, sides, width):
    for axis, dim in sides:
        count = lax.axis_size(axis)
        forward = [(i, i + 1) for i in range(count - 1)]
        backward = [(target, source) for source, target in forward]
        low = lax.ppermute(
            lax.slice_in_dim(block, block.shape[dim] - width, None, axis=dim), axis, forward
        )
        high = lax.ppermute(lax.slice_in_dim(block, 0, width, axis=dim), axis, backward)
        block = jnp.concatenate([low, block, high], axis=dim)
    return block


def lobatto_diff():
    points = [-1.0, -1.0 / math.sqrt(5.0), 1.0 / math.sqrt(5.0), 1.0]
    weights = [
        1.0 / math.prod([points[target] - points[other] for other in range(4) if other != target])
        for target in range(4)
    ]
    offdiag = [
        [
            (
                0.0
                if target == source
                else weights[source] / weights[target] / (points[target] - points[source])
            )
            for source in range(4)
        ]
        for target in range(4)
    ]
    return np.array(
        [
            [
                -sum(offdiag[target]) if target == source else offdiag[target][source]
                for source in range(4)
            ]
            for target in range(4)
        ],
        dtype=np.float32,
    )


def deriv_table():
    matrix = lobatto_diff()
    identity = np.eye(4, dtype=np.float32)
    return np.concatenate(
        [
            np.kron(np.kron(matrix, identity), identity),
            np.kron(np.kron(identity, matrix), identity),
            np.kron(np.kron(identity, identity), matrix),
        ],
        axis=0,
    ).astype(np.float32)


def face_table():
    entries = []
    for face_node in range(16):
        first_index = face_node // 4
        second_index = face_node % 4
        layout = []
        for face_id in range(6):
            coordinates = [first_index, second_index]
            coordinates.insert(face_id // 2, 3 * (face_id % 2))
            layout.append(16 * coordinates[0] + 4 * coordinates[1] + coordinates[2])
        entries.append(layout)
    return np.array(entries, dtype=np.int32)


def normal_table():
    return np.array(
        [
            [face_id % 2 * 2 - 1.0 if face_id // 2 == direction else 0.0 for face_id in range(6)]
            for direction in range(3)
        ],
        dtype=np.float32,
    )


def lift_table():
    nodes_of = face_table()
    return np.array(
        [
            [
                lift_weight if nodes_of[column // 6, column % 6] == node_id else 0.0
                for column in range(96)
            ]
            for node_id in range(64)
        ],
        dtype=np.float32,
    )


def normal_parts():
    normals = jnp.asarray(normal_table())
    return normals[:, None, :, None]


def lift_apply(face_terms):
    matrix = jnp.asarray(lift_table())
    components = face_terms.shape[0]
    return jnp.einsum(
        "nm,cme->cne",
        matrix,
        face_terms.reshape(components, 96, face_terms.shape[-1]),
        precision=lax.Precision.HIGHEST,
    )


def stress_faces(velocity_jump, lame_face, shear_face):
    shaped = normal_parts()
    along = (
        velocity_jump[0] * shaped[0] + velocity_jump[1] * shaped[1] + velocity_jump[2] * shaped[2]
    )
    pieces = []
    for first, second in component_pairs:
        shear_part = shear_face * (
            velocity_jump[first] * shaped[second] + velocity_jump[second] * shaped[first]
        )
        if first == second:
            pieces.append(0.5 * (lame_face * along + shear_part))
        else:
            pieces.append(0.5 * shear_part)
    return jnp.stack(pieces)


def traction_of(traces):
    shaped = normal_parts()
    return jnp.stack(
        [
            traces[symmetric_index[component][0]] * shaped[0]
            + traces[symmetric_index[component][1]] * shaped[1]
            + traces[symmetric_index[component][2]] * shaped[2]
            for component in range(3)
        ]
    )


def stress_rate(gradient, lame_first, shear_mod):
    trace_sum = gradient[0, 0] + gradient[1, 1] + gradient[2, 2]
    pieces = []
    for first, second in component_pairs:
        shear_part = shear_mod * (gradient[first, second] + gradient[second, first])
        if first == second:
            pieces.append(lame_first * trace_sum + shear_part)
        else:
            pieces.append(shear_part)
    return jnp.stack(pieces)


def divergence(stress_grad):
    return jnp.stack(
        [
            stress_grad[symmetric_index[component][0], 0]
            + stress_grad[symmetric_index[component][1], 1]
            + stress_grad[symmetric_index[component][2], 2]
            for component in range(3)
        ]
    )


def kernel_terms(forward, velocity, stress, forward_grad):
    rho_term = -time_step * (
        forward[0] * velocity[0] + forward[1] * velocity[1] + forward[2] * velocity[2]
    )
    trace_rate = forward_grad[0, 0] + forward_grad[1, 1] + forward_grad[2, 2]
    lame_term = -time_step * trace_rate * (stress[0] + stress[1] + stress[2])
    contraction = 0.0
    for first in range(3):
        for second in range(3):
            contraction = (
                contraction
                + 0.5
                * (forward_grad[first, second] + forward_grad[second, first])
                * stress[symmetric_index[first][second]]
            )
    shear_term = -time_step * 2.0 * contraction
    return jnp.stack([rho_term, lame_term, shear_term])


def volume_grad(nodal_field, deriv_stack):
    components = nodal_field.shape[0]
    stacked = jnp.einsum("an,cne->cae", deriv_stack, nodal_field, precision=lax.Precision.HIGHEST)
    return stacked.reshape(components, 3, 64, nodal_field.shape[-1])


def outgoing_faces(traces, send_index):
    trace_cols = traces.reshape(traces.shape[0] * traces.shape[1], -1)
    return (trace_cols, jnp.take(trace_cols, send_index, axis=1))


def partner_faces(trace_cols, received, partner, shape):
    combined = jnp.concatenate([trace_cols, received[:, 0], received[:, 3]], axis=1)
    return jnp.take(combined, partner, axis=1).reshape(shape)


def local(
    adjoint_state, forward_velocity, density, lame_lambda, shear_modulus, neighbour, send_list
):
    slot_count = density.shape[1]
    nodes_of = face_table()
    deriv_stack = jnp.asarray(deriv_table())
    event_state = adjoint_state[0]
    forward = forward_velocity[0]
    valid_mask = jnp.any(neighbour >= 0, axis=0).astype(jnp.float32)[None]
    face_ids = lax.broadcasted_iota(jnp.int32, neighbour.shape, 0)
    slot_ids = lax.broadcasted_iota(jnp.int32, neighbour.shape, 1)
    own_key = face_ids * slot_count + slot_ids
    partner = jnp.where(
        neighbour < 0,
        own_key,
        jnp.where(
            neighbour < slot_count,
            (face_ids ^ 1) * slot_count + neighbour,
            5 * slot_count + neighbour,
        ),
    ).reshape(-1)
    outer_sign = jnp.where(neighbour < 0, -1.0, 1.0).astype(jnp.float32)[None, None]
    send_index = jnp.maximum(send_list, 0)
    lame_face = lame_lambda[nodes_of]
    shear_face = shear_modulus[nodes_of]
    impedance = jnp.sqrt(density[nodes_of] * (lame_face + 2.0 * shear_face))
    velocity = event_state[0:3] * valid_mask
    stress = event_state[3:9] * valid_mask
    kernel_whole = jnp.zeros((3, 64 * slot_count), jnp.float32)
    for step in range(forward.shape[0]):
        vel_traces = velocity[:, nodes_of]
        vel_cols, vel_out = outgoing_faces(vel_traces, send_index)
        vel_in = with_halo(vel_out, (("dom", 1),), 1)
        velocity_jump = partner_faces(vel_cols, vel_in, partner, vel_traces.shape) - vel_traces
        vel_grad = volume_grad(velocity, deriv_stack)
        stress = stress + time_step * (
            stress_rate(vel_grad, lame_lambda, shear_modulus)
            + lift_apply(stress_faces(velocity_jump, lame_face, shear_face))
        )
        str_traces = stress[:, nodes_of]
        own_traction = traction_of(str_traces)
        str_cols, str_out = outgoing_faces(str_traces, send_index)
        str_in = with_halo(str_out, (("dom", 1),), 1)
        plus_stress = partner_faces(str_cols, str_in, partner, str_traces.shape) * outer_sign
        plus_traction = traction_of(plus_stress)
        traction_jump = plus_traction - own_traction
        vel_faces = 0.5 * traction_jump + 0.5 * impedance * velocity_jump
        velocity = velocity + time_step / density * (
            divergence(volume_grad(stress, deriv_stack)) + lift_apply(vel_faces)
        )
        step_terms = kernel_terms(
            forward[step], velocity, stress, volume_grad(forward[step], deriv_stack)
        ).reshape(3, -1)
        kernel_whole = kernel_whole + lax.psum(step_terms, "event")
    share_width = kernel_whole.shape[1] // lax.axis_size("event")
    kernel_part = lax.dynamic_slice_in_dim(
        kernel_whole, lax.axis_index("event") * share_width, share_width, 1
    )
    return (velocity[None], kernel_part.reshape(3, 1, -1))


def solution(mesh):
    placed = (
        P("event", None, None, "dom"),
        P("event", None, None, None, "dom"),
        P(None, "dom"),
        P(None, "dom"),
        P(None, "dom"),
        P(None, "dom"),
        P(None, "dom"),
    )
    return jax.shard_map(
        local,
        mesh=mesh,
        in_specs=placed,
        out_specs=(P("event", None, None, "dom"), P(None, "dom", "event")),
        check_vma=False,
    )
```

profile of v0, /device:TPU:8, one launch (start us, length us, event | category | flops | bytes accessed | tf_op | source)
XLA Modules:
  0.0 640.6 jit_solution(9028134080841680794)
XLA Ops:
  16.6 3.6 gather_fusion.9
  23.0 3.6 collective-permute-start.1
  29.0 2.9 fusion.235
  34.7 2.8 fusion.63
  37.5 2.8 fusion.65
  53.5 9.3 %gather_fusion.10 = f32[4608,48]{1,0:T(8,128)} fusion(f32[48,5488]{0,1:T(8,128)S(1)} %copy.174, s32[5120]{0:T(1024)S(1)} %pad_clamp_fusion), kind=kCustom, calls=%fused_computation.1.clone | custom fusion | bytes 1787904 | tf_op jit(solution)/shard_map/jit(_take)/gather | solution.py:208
  62.7 3.8 select_bitcast_fusion.5
  85.3 4.8 fusion.236
  109.4 9.3 %collective-permute-start.3 = (f32[96,1,440]{0,2,1:T(8,128)S(1)}, f32[96,1,440]{0,2,1:T(8,128)S(1)}, u32[]{:S(2)}, u32[]{:S(2)}) collective-permute-start(f32[96,1,440]{0,2,1:T(8,128)S(1)} %get-tuple-element.80), channel_id=1, source_target_pairs={{48,0},{96,48},{144,96},{192,144},{240,192},{288,240},{336,288},{3... | collective-permute-start | bytes 506888 | tf_op jit(solution)/shard_map/ppermute | solution.py:23
  129.2 9.3 %gather_fusion.12 = f32[4608,96]{1,0:T(8,128)} fusion(f32[96,5488]{0,1:T(8,128)S(1)} %pad_maximum_fusion, s32[5120]{0:T(1024)S(1)} %pad_clamp_fusion), kind=kCustom, calls=%fused_computation.3.clone | custom fusion | bytes 3557376 | tf_op jit(solution)/shard_map/jit(_take)/gather | solution.py:208
  138.4 3.8 select_bitcast_fusion.4
  156.6 2.8 fusion.237
  162.2 2.8 copy.196
  165.0 3.6 gather_fusion.13
  170.9 4.0 collective-permute-start.5
  183.0 9.3 %gather_fusion.14 = f32[4608,48]{1,0:T(8,128)} fusion(f32[48,5488]{0,1:T(8,128)S(1)} %copy.198, s32[5120]{0:T(1024)S(1)} %pad_clamp_fusion), kind=kCustom, calls=%fused_computation.6.clone | custom fusion | bytes 1787904 | tf_op jit(solution)/shard_map/jit(_take)/gather | solution.py:208
  192.3 3.8 select_bitcast_fusion.3
  209.1 2.9 fusion.7
  212.8 4.8 fusion.238
  236.9 3.8 collective-permute-start.7
  251.1 9.3 %gather_fusion.16 = f32[4608,96]{1,0:T(8,128)} fusion(f32[96,5488]{0,1:T(8,128)S(1)} %pad_maximum_fusion.1, s32[5120]{0:T(1024)S(1)} %pad_clamp_fusion), kind=kCustom, calls=%fused_computation.10.clone | custom fusion | bytes 3557376 | tf_op jit(solution)/shard_map/jit(_take)/gather | solution.py:208
  260.4 3.8 select_bitcast_fusion.2
  292.9 3.9 collective-permute-start.9
  305.1 9.3 %gather_fusion.18 = f32[4608,48]{1,0:T(8,128)} fusion(f32[48,5488]{0,1:T(8,128)S(1)} %copy.222, s32[5120]{0:T(1024)S(1)} %pad_clamp_fusion), kind=kCustom, calls=%fused_computation.7.clone | custom fusion | bytes 1787904 | tf_op jit(solution)/shard_map/jit(_take)/gather | solution.py:208
  314.4 3.8 select_bitcast_fusion.1
  333.7 2.9 fusion.8
  338.6 4.8 fusion.240
  359.5 3.9 collective-permute-start.11
  373.7 9.3 %gather_fusion.20 = f32[4608,96]{1,0:T(8,128)} fusion(f32[96,5488]{0,1:T(8,128)S(1)} %pad_maximum_fusion.2, s32[5120]{0:T(1024)S(1)} %pad_clamp_fusion), kind=kCustom, calls=%fused_computation.11.clone | custom fusion | bytes 3557376 | tf_op jit(solution)/shard_map/jit(_take)/gather | solution.py:208
  383.0 3.8 select_bitcast_fusion
  393.2 3.2 fusion.11
  400.4 231.6 %all-reduce.2.cloned.1.call-done = f32[3,49152]{1,0:T(4,128)} async-done(((f32[3,49152]{1,0:T(4,128)}), f32[3,49152]{1,0:T(4,128)}) %all-reduce.2.cloned.1.call-update) | async-done | bytes 589840 | tf_op jit(solution)/shard_map/psum | solution.py:264
  (475 shorter events, 240.7 us)
Async XLA Ops:
  7.2 624.9 %all-reduce.2.cloned.1.call-start = ((), (), s32[]{:S(2)}) async-start(), calls=%async_computation | async-start | bytes 1572864 | tf_op jit(solution)/shard_map/psum | solution.py:264
  8.6 11.7 %copy-start.90 = (pred[2,440]{1,0:T(4,128)(4,1)}, pred[2,440]{1,0:T(4,128)(4,1)S(1)}, u32[]{:S(2)}) copy-start(pred[2,440]{1,0:T(4,128)(4,1)S(1)} %broadcast_compare_fusion.1) | copy-start | bytes 2644
  10.6 18.4 %copy-start.31 = (f32[3,64,768]{2,1,0:T(8,128)}, f32[3,64,768]{2,1,0:T(8,128)S(1)}, u32[]{:S(2)}) copy-start(f32[3,64,768]{2,1,0:T(8,128)S(1)} %bitcast_multiply_fusion.1) | copy-start | bytes 1769476
  16.5 10.1 %copy-start.85 = (s32[6,768]{1,0:T(8,128)S(1)}, s32[6,768]{1,0:T(8,128)}, u32[]{:S(2)}) copy-start(s32[6,768]{1,0:T(8,128)} %param.46) | copy-start | bytes 55300
  16.5 10.2 %copy-start.2 = (f32[64,768]{1,0:T(8,128)S(1)}, f32[64,768]{1,0:T(8,128)}, u32[]{:S(2)}) copy-start(f32[64,768]{1,0:T(8,128)} %param.43) | copy-start | bytes 589828
  21.1 27.9 %collective-permute-start = (f32[48,1,440]{2,0,1:T(8,128)}, f32[48,1,440]{2,0,1:T(8,128)S(1)}, u32[]{:S(2)}, u32[]{:S(2)}) collective-permute-start(f32[48,1,440]{2,0,1:T(8,128)} %get-tuple-element.86), channel_id=1, source_target_pairs={{0,48},{48,96},{96,144},{144,192},{192,240},{240,288},{288,336},{3... | collective-permute-start | bytes 253448 | tf_op jit(solution)/shard_map/ppermute | solution.py:20
  23.0 26.0 %collective-permute-start.1 = (f32[48,1,440]{2,0,1:T(8,128)}, f32[48,1,440]{2,0,1:T(8,128)}, u32[]{:S(2)}, u32[]{:S(2)}) collective-permute-start(f32[48,1,440]{2,0,1:T(8,128)} %get-tuple-element.85), channel_id=1, source_target_pairs={{48,0},{96,48},{144,96},{192,144},{240,192},{288,240},{336,288},{3... | collective-permute-start | bytes 253448 | tf_op jit(solution)/shard_map/ppermute | solution.py:23
  84.6 9.7 %copy-start.5 = (f32[6,64,768]{2,1,0:T(8,128)}, f32[6,64,768]{2,1,0:T(8,128)S(1)}, u32[]{:S(2)}) copy-start(f32[6,64,768]{2,1,0:T(8,128)S(1)} %fusion.6) | copy-start | bytes 3538948
  106.5 12.2 %copy-start.95 = (f32[6]{0:T(128)S(1)}, f32[6]{0:T(128)}, u32[]{:S(2)}) copy-start(f32[6]{0:T(128)} %constant.39) | copy-start | bytes 76
  106.6 12.2 %copy-start.103 = (f32[6]{0:T(128)S(1)}, f32[6]{0:T(128)}, u32[]{:S(2)}) copy-start(f32[6]{0:T(128)} %constant.51) | copy-start | bytes 76
  106.6 12.2 %copy-start.111 = (f32[6]{0:T(128)S(1)}, f32[6]{0:T(128)}, u32[]{:S(2)}) copy-start(f32[6]{0:T(128)} %constant.102) | copy-start | bytes 76
  107.5 19.6 %collective-permute-start.2 = (f32[96,1,440]{0,2,1:T(8,128)S(1)}, f32[96,1,440]{0,2,1:T(8,128)S(1)}, u32[]{:S(2)}, u32[]{:S(2)}) collective-permute-start(f32[96,1,440]{0,2,1:T(8,128)S(1)} %get-tuple-element.79), channel_id=1, source_target_pairs={{0,48},{48,96},{96,144},{144,192},{192,240},{240,288},{288,336},{3... | collective-permute-start | bytes 506888 | tf_op jit(solution)/shard_map/ppermute | solution.py:20
  109.4 17.7 %collective-permute-start.3 = (f32[96,1,440]{0,2,1:T(8,128)S(1)}, f32[96,1,440]{0,2,1:T(8,128)S(1)}, u32[]{:S(2)}, u32[]{:S(2)}) collective-permute-start(f32[96,1,440]{0,2,1:T(8,128)S(1)} %get-tuple-element.80), channel_id=1, source_target_pairs={{48,0},{96,48},{144,96},{192,144},{240,192},{288,240},{336,288},{3... | collective-permute-start | bytes 506888 | tf_op jit(solution)/shard_map/ppermute | solution.py:23
  146.6 6.6 %copy-start.51 = (f32[3,96,768]{2,1,0:T(8,128)S(1)}, f32[3,96,768]{2,1,0:T(8,128)}, u32[]{:S(2)}) copy-start(f32[3,96,768]{2,1,0:T(8,128)} %gather.56) | copy-start | bytes 2654212
  168.8 8.3 %copy-start.33 = (f32[3,768,192]{1,2,0:T(8,128)S(1)}, f32[3,768,192]{1,2,0:T(8,128)}, u32[]{:S(2)}) copy-start(f32[3,768,192]{1,2,0:T(8,128)} %fusion.237) | copy-start | bytes 5308420
  168.8 10.6 %collective-permute-start.4 = (f32[48,1,440]{2,0,1:T(8,128)S(1)}, f32[48,1,440]{2,0,1:T(8,128)S(1)}, u32[]{:S(2)}, u32[]{:S(2)}) collective-permute-start(f32[48,1,440]{2,0,1:T(8,128)S(1)} %get-tuple-element.84), channel_id=1, source_target_pairs={{0,48},{48,96},{96,144},{144,192},{192,240},{240,288},{288,336},{3... | collective-permute-start | bytes 253448 | tf_op jit(solution)/shard_map/ppermute | solution.py:20
  170.9 8.5 %collective-permute-start.5 = (f32[48,1,440]{2,0,1:T(8,128)S(1)}, f32[48,1,440]{2,0,1:T(8,128)S(1)}, u32[]{:S(2)}, u32[]{:S(2)}) collective-permute-start(f32[48,1,440]{2,0,1:T(8,128)S(1)} %get-tuple-element.83), channel_id=1, source_target_pairs={{48,0},{96,48},{144,96},{192,144},{240,192},{288,240},{336,288},{3... | collective-permute-start | bytes 253448 | tf_op jit(solution)/shard_map/ppermute | solution.py:23
  203.4 5.7 copy-start.6
  212.0 9.7 %copy-start.3 = (f32[6,64,768]{2,1,0:T(8,128)}, f32[6,64,768]{2,1,0:T(8,128)S(1)}, u32[]{:S(2)}) copy-start(f32[6,64,768]{2,1,0:T(8,128)S(1)} %fusion.7) | copy-start | bytes 3538948
  234.0 6.7 %copy-start.98 = (f32[6]{0:T(128)S(1)}, f32[6]{0:T(128)}, u32[]{:S(2)}) copy-start(f32[6]{0:T(128)} %constant.39) | copy-start | bytes 76
  234.0 6.7 %copy-start.106 = (f32[6]{0:T(128)S(1)}, f32[6]{0:T(128)}, u32[]{:S(2)}) copy-start(f32[6]{0:T(128)} %constant.51) | copy-start | bytes 76
  234.0 6.7 %copy-start.114 = (f32[6]{0:T(128)S(1)}, f32[6]{0:T(128)}, u32[]{:S(2)}) copy-start(f32[6]{0:T(128)} %constant.102) | copy-start | bytes 76
  234.9 14.1 %collective-permute-start.6 = (f32[96,1,440]{0,2,1:T(8,128)S(1)}, f32[96,1,440]{0,2,1:T(8,128)S(1)}, u32[]{:S(2)}, u32[]{:S(2)}) collective-permute-start(f32[96,1,440]{0,2,1:T(8,128)S(1)} %get-tuple-element.77), channel_id=1, source_target_pairs={{0,48},{48,96},{96,144},{144,192},{192,240},{240,288},{288,336},{3... | collective-permute-start | bytes 506888 | tf_op jit(solution)/shard_map/ppermute | solution.py:20
  236.9 12.2 %collective-permute-start.7 = (f32[96,1,440]{0,2,1:T(8,128)S(1)}, f32[96,1,440]{0,2,1:T(8,128)S(1)}, u32[]{:S(2)}, u32[]{:S(2)}) collective-permute-start(f32[96,1,440]{0,2,1:T(8,128)S(1)} %get-tuple-element.78), channel_id=1, source_target_pairs={{48,0},{96,48},{144,96},{192,144},{240,192},{288,240},{336,288},{3... | collective-permute-start | bytes 506888 | tf_op jit(solution)/shard_map/ppermute | solution.py:23
  290.7 8.1 %copy-start.34 = (f32[3,768,192]{1,2,0:T(8,128)S(1)}, f32[3,768,192]{1,2,0:T(8,128)}, u32[]{:S(2)}) copy-start(f32[3,768,192]{1,2,0:T(8,128)} %fusion.239) | copy-start | bytes 5308420
  290.8 10.8 %collective-permute-start.8 = (f32[48,1,440]{2,0,1:T(8,128)S(1)}, f32[48,1,440]{2,0,1:T(8,128)S(1)}, u32[]{:S(2)}, u32[]{:S(2)}) collective-permute-start(f32[48,1,440]{2,0,1:T(8,128)S(1)} %get-tuple-element.82), channel_id=1, source_target_pairs={{0,48},{48,96},{96,144},{144,192},{192,240},{240,288},{288,336},{3... | collective-permute-start | bytes 253448 | tf_op jit(solution)/shard_map/ppermute | solution.py:20
  292.9 8.7 %collective-permute-start.9 = (f32[48,1,440]{2,0,1:T(8,128)S(1)}, f32[48,1,440]{2,0,1:T(8,128)S(1)}, u32[]{:S(2)}, u32[]{:S(2)}) collective-permute-start(f32[48,1,440]{2,0,1:T(8,128)S(1)} %get-tuple-element.81), channel_id=1, source_target_pairs={{48,0},{96,48},{144,96},{192,144},{240,192},{288,240},{336,288},{3... | collective-permute-start | bytes 253448 | tf_op jit(solution)/shard_map/ppermute | solution.py:23
  357.3 6.1 copy-start.101
  357.3 6.1 copy-start.109
  357.3 6.1 copy-start.117
  357.6 14.1 %collective-permute-start.10 = (f32[96,1,440]{0,2,1:T(8,128)S(1)}, f32[96,1,440]{0,2,1:T(8,128)S(1)}, u32[]{:S(2)}, u32[]{:S(2)}) collective-permute-start(f32[96,1,440]{0,2,1:T(8,128)S(1)} %get-tuple-element.75), channel_id=1, source_target_pairs={{0,48},{48,96},{96,144},{144,192},{192,240},{240,288},{288,336},{3... | collective-permute-start | bytes 506888 | tf_op jit(solution)/shard_map/ppermute | solution.py:20
  359.5 12.2 %collective-permute-start.11 = (f32[96,1,440]{0,2,1:T(8,128)S(1)}, f32[96,1,440]{0,2,1:T(8,128)S(1)}, u32[]{:S(2)}, u32[]{:S(2)}) collective-permute-start(f32[96,1,440]{0,2,1:T(8,128)S(1)} %get-tuple-element.76), channel_id=1, source_target_pairs={{48,0},{96,48},{144,96},{192,144},{240,192},{288,240},{336,288},{3... | collective-permute-start | bytes 506888 | tf_op jit(solution)/shard_map/ppermute | solution.py:23
  (102 other events, 236.1 us)
Sparse Core Ops, SparseCore 0:
  400.5 231.4 all-reduce.1
where the time goes:
time: 651 us; the launch traced here: 641 us
  waiting for transfers between devices  232 us (36%)
  local copies, waits for them, and re-layouts  228 us (35%)
  other arithmetic  76 us (12%)
  matrix products  48.5 us (7%)
  starting transfers between devices  40.4 us (6%)
  between operations  16.4 us (3%)
    psum x1, waiting for transfers between devices, local(): kernel_whole = kernel_whole + lax.psum(step_terms, 'event')  232 us
    gather x6, local copies, waits for them, and re-layouts, partner_faces(): return jnp.take(combined, partner, axis=1).reshape(shape)  55.6 us
    unnamed x272, local copies, waits for them, and re-layouts  41 us
    dot_general x9, matrix products, volume_grad(): jnp.einsum('an,cne->cae', deriv_stack, nodal_field, precision=lax.Precisi...  31.4 us
    ppermute x6, starting transfers between devices, with_halo(): lax.ppermute(lax.slice_in_dim(block, 0, width, axis=dim), axis, backward)  28.6 us
    select_n x7, other arithmetic, partner_faces(): return jnp.take(combined, partner, axis=1).reshape(shape)  22.9 us
    unnamed x22, other arithmetic  18.5 us
    another operation x18, local copies, waits for them, and re-layouts, traction_of(): jnp.stack([traces[symmetric_index[component][0]] * shaped[0] + traces[sym...  18 us
  transfers between devices with their start and end apart: 13, of which 1 were waited for; matrix products, arithmetic and copies ran while one was open for 8% of the time, Pallas kernels for 0%

commit v1 on v0

v1 whole, which is shorter than its diff:
```python
import functools
import math

import jax
import jax.numpy as jnp
import numpy as np
from jax import lax
from jax.experimental import pallas as pl
from jax.experimental.pallas import tpu as pltpu
from jax.sharding import PartitionSpec as P
import ml_dtypes

time_step = 0.02
half_lift = 3.0
symmetric_index = ((0, 3, 4), (3, 1, 5), (4, 5, 2))
SIDE = 512
MESH = pl.DeviceIdType.MESH
f32 = jnp.float32
bf16 = jnp.bfloat16


def lobatto_diff():
    points = [-1.0, -1.0 / math.sqrt(5.0), 1.0 / math.sqrt(5.0), 1.0]
    weights = [
        1.0 / math.prod([points[target] - points[other] for other in range(4) if other != target])
        for target in range(4)
    ]
    offdiag = [
        [
            (
                0.0
                if target == source
                else weights[source] / weights[target] / (points[target] - points[source])
            )
            for source in range(4)
        ]
        for target in range(4)
    ]
    return np.array(
        [
            [
                -sum(offdiag[target]) if target == source else offdiag[target][source]
                for source in range(4)
            ]
            for target in range(4)
        ],
        dtype=np.float32,
    )


def deriv_table():
    matrix = lobatto_diff()
    identity = np.eye(4, dtype=np.float32)
    return np.concatenate(
        [
            np.kron(np.kron(matrix, identity), identity),
            np.kron(np.kron(identity, matrix), identity),
            np.kron(np.kron(identity, identity), matrix),
        ],
        axis=0,
    ).astype(np.float32)


def face_nodes():
    nodes = np.zeros((6, 16), np.int32)
    for face in range(6):
        for q in range(16):
            coordinates = [q // 4, q % 4]
            coordinates.insert(face // 2, 3 * (face % 2))
            nodes[face, q] = 16 * coordinates[0] + 4 * coordinates[1] + coordinates[2]
    return nodes


def tables():
    to_bf16 = lambda x: np.asarray(x, np.float32).astype(ml_dtypes.bfloat16)
    deriv = deriv_table()
    high = to_bf16(deriv)
    low = to_bf16(deriv - high.astype(np.float32))
    deriv3 = np.concatenate([high, low, high], axis=1)
    nodes = face_nodes()
    extract = np.zeros((96, 64), np.float32)
    signed = np.zeros((192, 96), np.float32)
    summed = np.zeros((64, 96), np.float32)
    plain = np.zeros((64, 96), np.float32)
    for face in range(6):
        sign = face % 2 * 2 - 1.0
        for q in range(16):
            column, node = face * 16 + q, nodes[face, q]
            extract[column, node] = 1.0
            signed[face // 2 * 64 + node, column] = half_lift * sign
            summed[node, column] = half_lift * sign
            plain[node, column] = half_lift
    grad_rows = np.concatenate([deriv3.astype(np.float32), signed, signed], axis=1)
    jump_rows = np.concatenate([np.zeros((64, 192), np.float32), plain, plain], axis=1)
    stage_a = np.concatenate([grad_rows, jump_rows], axis=0)
    lift2 = np.concatenate([summed, summed], axis=1)
    return to_bf16(stage_a), deriv3, to_bf16(lift2), to_bf16(extract)


def split(x):
    high = x.astype(bf16)
    return high, (x - high.astype(f32)).astype(bf16)


def dot(a, b):
    return jnp.dot(a, b, preferred_element_type=f32)


def sim_kernel(
    state, forward, rho, lam, mu, near, sends, stage_a, deriv3, lift2, extract,
    vel, acc,
    sig, onehot, pick, send_ids, traces, jump, grad_in, grad, fgrad, sig_in, jump_in, impulse, div,
    halves, out_buf, in_buf, send_sem, recv_sem,
):
    count = lax.axis_size("dom")
    me = lax.axis_index("dom")
    lower = lax.rem(me + count - 1, count)
    upper = lax.rem(me + 1, count)
    slots = rho.shape[1]
    cap = sends.shape[1]
    top = slots + 2 * SIDE
    steps = forward.shape[1]

    barrier = pltpu.get_barrier_semaphore()
    for other in (lower, upper):
        pl.semaphore_signal(barrier, inc=1, device_id={"dom": other}, device_id_type=MESH)

    valid = jnp.where(jnp.max(near[...], axis=0, keepdims=True) >= 0, 1.0, 0.0)
    for c in range(3):
        vel[0, c] = state[0, c] * valid
    for c in range(6):
        sig[c] = state[0, 3 + c] * valid
    acc[...] = jnp.zeros_like(acc)

    send_ids[...] = jnp.full_like(send_ids, -1)
    send_ids[0:1, 0:cap] = sends[0:1, :]
    send_ids[0:1, SIDE : SIDE + cap] = sends[1:2, :]
    ids = send_ids[0:1, :]
    face_of = jnp.where(ids < 0, -1, 0)
    for f in range(1, 6):
        face_of = face_of + jnp.where(ids >= f * slots, 1, 0)
    slot_of = ids - face_of * slots
    slot_of = jnp.where(ids < 0, -1, slot_of)

    def build_pick(k, carry):
        rows = pl.ds(pl.multiple_of(k * 64, 64), 64)
        index = lax.broadcasted_iota(jnp.int32, (64, 2 * SIDE), 0) + k * 64
        pick[rows, :] = jnp.where(index == slot_of, 1.0, 0.0).astype(bf16)
        return carry

    lax.fori_loop(0, slots // 64, build_pick, 0)

    def inner_of(f):
        return jnp.where(near[f : f + 1, :] >= 0, 1.0, 0.0)

    def copies(phase):
        return [
            pltpu.make_async_remote_copy(
                src_ref=out_buf.at[phase, side],
                dst_ref=in_buf.at[phase, 1 - side],
                send_sem=send_sem.at[phase, side],
                recv_sem=recv_sem.at[phase, 1 - side],
                device_id={"dom": other},
                device_id_type=MESH,
            )
            for side, other in ((0, lower), (1, upper))
        ]

    def send(phase):
        rows = traces[...].reshape(576, slots)
        for side in range(2):
            for part in range(SIDE // 256):
                start = side * SIDE + part * 256
                got = dot(rows, pick[:, start : start + 256])
                face = face_of[:, start : start + 256]
                total = jnp.zeros((48, 256), f32)
                for f in range(6):
                    both = got[f * 96 : f * 96 + 48] + got[f * 96 + 48 : f * 96 + 96]
                    total = jnp.where(face == f, both, total)
                out_buf[phase, side, :, part * 256 : part * 256 + 256] = total
        for copy in copies(phase):
            copy.start()

    def own(phase):
        for f in range(6):
            got = dot(traces[f ^ 1], onehot[f, 0:slots, :])
            mine = traces[f, 0:48].astype(f32) + traces[f, 48:96].astype(f32)
            weight = inner_of(f) if phase == 0 else 2.0 - inner_of(f)
            jump[f] = got[0:48] + got[48:96] - mine * weight

    def arrive(phase, target, base):
        for copy in copies(phase):
            copy.wait()
        for side in range(2):
            high, low = split(in_buf[phase, side])
            halves[0:48, side * SIDE : side * SIDE + SIDE] = high
            halves[48:96, side * SIDE : side * SIDE + SIDE] = low
        for f in range(6):
            got = dot(halves[...], onehot[f, slots:top, :])
            high, low = split(jump[f] + got[0:48] + got[48:96])
            for c in range(3):
                target[c, base + f * 16 : base + f * 16 + 16] = high[c * 16 : c * 16 + 16]
                target[c, base + 96 + f * 16 : base + 112 + f * 16] = low[c * 16 : c * 16 + 16]

    def put3(ref, index, high, low):
        ref[index, 0:64] = high
        ref[index, 64:128] = high
        ref[index, 128:192] = low

    def velocity_traces():
        for c in range(3):
            high, low = split(vel[0, c])
            put3(grad_in, c, high, low)
            for part, x in enumerate((high, low)):
                got = dot(extract[...], x).astype(bf16)
                for f in range(6):
                    at = part * 48 + c * 16
                    traces[f, at : at + 16] = got[f * 16 : f * 16 + 16]

    def stress_traces():
        for m, pairs in enumerate(
            (((0, 0),), ((1, 1),), ((2, 2),), ((1, 0), (0, 1)), ((2, 0), (0, 2)), ((2, 1), (1, 2)))
        ):
            high, low = split(sig[m])
            put3(sig_in, m, high, low)
            for part, x in enumerate((high, low)):
                for c, d in pairs:
                    got = dot(extract[d * 32 : d * 32 + 32, :], x).astype(bf16)
                    for end in range(2):
                        at = part * 48 + c * 16
                        traces[2 * d + end, at : at + 16] = got[end * 16 : end * 16 + 16]

    def build_onehot():
        for f in range(6):
            code = near[f : f + 1, :]
            code = jnp.where(code >= slots + cap, code + (SIDE - cap), code)

            def body(k, carry):
                rows = pl.ds(pl.multiple_of(k * 64, 64), 64)
                index = lax.broadcasted_iota(jnp.int32, (64, slots), 0) + k * 64
                onehot[f, rows, :] = jnp.where(index == code, 1.0, 0.0).astype(bf16)
                return carry

            lax.fori_loop(0, top // 64, body, 0)

    def step(n, carry):
        velocity_traces()

        @pl.when(n == 0)
        def _():
            pl.semaphore_wait(barrier, 2)

        send(0)

        @pl.when(n == 0)
        def _():
            build_onehot()

        own(0)
        for c in range(3):
            high, low = split(forward[0, n, c])
            stack = jnp.concatenate([high, high, low], axis=0)
            fgrad[c] = dot(deriv3[...], stack)
        arrive(0, grad_in, 192)
        for c in range(3):
            grad[c] = dot(stage_a[...], grad_in[c])
        for r in range(0, 64, 16):
            rows = slice(r, r + 16)
            g = [[grad[i, j * 64 + r : j * 64 + r + 16] for j in range(3)] for i in range(3)]
            shear = mu[rows] * time_step
            bulk = lam[rows] * time_step * (g[0][0] + g[1][1] + g[2][2])
            for c in range(3):
                sig[c, rows] = sig[c, rows] + (bulk + 2.0 * shear * g[c][c])
            for m, (i, j) in ((3, (0, 1)), (4, (0, 2)), (5, (1, 2))):
                sig[m, rows] = sig[m, rows] + shear * (g[i][j] + g[j][i])
        stress_traces()
        send(1)
        own(1)
        for c in range(3):
            total = dot(deriv3[0:64], sig_in[symmetric_index[c][0]])
            total = total + dot(deriv3[64:128], sig_in[symmetric_index[c][1]])
            total = total + dot(deriv3[128:192], sig_in[symmetric_index[c][2]])
            div[c] = total
        for r in range(0, 64, 16):
            rows = slice(r, r + 16)
            g = [[fgrad[i, j * 64 + r : j * 64 + r + 16] for j in range(3)] for i in range(3)]
            s = [sig[m, rows] for m in range(6)]
            rate = g[0][0] + g[1][1] + g[2][2]
            acc[1, rows] = acc[1, rows] - time_step * rate * (s[0] + s[1] + s[2])
            contraction = g[0][0] * s[0] + g[1][1] * s[1] + g[2][2] * s[2]
            contraction = contraction + (g[0][1] + g[1][0]) * s[3]
            contraction = contraction + (g[0][2] + g[2][0]) * s[4]
            contraction = contraction + (g[1][2] + g[2][1]) * s[5]
            acc[2, rows] = acc[2, rows] - (2.0 * time_step) * contraction
        arrive(1, jump_in, 0)
        for c in range(3):
            impulse[c] = dot(lift2[...], jump_in[c])
        for r in range(0, 64, 16):
            rows = slice(r, r + 16)
            z = jnp.sqrt(rho[rows] * (lam[rows] + 2.0 * mu[rows]))
            scale = time_step / rho[rows]
            total = jnp.zeros_like(z)
            for c in range(3):
                rate = div[c, rows] + impulse[c, rows] + z * grad[c, 192 + r : 192 + r + 16]
                new = vel[0, c, rows] + scale * rate
                vel[0, c, rows] = new
                total = total + forward[0, n, c, rows] * new
            acc[0, rows] = acc[0, rows] - time_step * total
        return carry

    lax.fori_loop(0, steps, step, 0)


def local(
    adjoint_state, forward_velocity, density, lame_lambda, shear_modulus, neighbour, send_list
):
    slots = density.shape[1]
    top = slots + 2 * SIDE
    stage_a, deriv3, lift2, extract = (jnp.asarray(x) for x in tables())
    vmem = pl.BlockSpec(memory_space=pltpu.VMEM)
    velocity, terms = pl.pallas_call(
        sim_kernel,
        out_shape=(
            jax.ShapeDtypeStruct((1, 3, 64, slots), f32),
            jax.ShapeDtypeStruct((3, 64, slots), f32),
        ),
        in_specs=[vmem] * 11,
        out_specs=(vmem, vmem),
        scratch_shapes=[
            pltpu.VMEM((6, 64, slots), f32),
            pltpu.VMEM((6, top, slots), bf16),
            pltpu.VMEM((slots, 2 * SIDE), bf16),
            pltpu.VMEM((8, 2 * SIDE), jnp.int32),
            pltpu.VMEM((6, 96, slots), bf16),
            pltpu.VMEM((6, 48, slots), f32),
            pltpu.VMEM((3, 384, slots), bf16),
            pltpu.VMEM((3, 256, slots), f32),
            pltpu.VMEM((3, 192, slots), f32),
            pltpu.VMEM((6, 192, slots), bf16),
            pltpu.VMEM((3, 192, slots), bf16),
            pltpu.VMEM((3, 64, slots), f32),
            pltpu.VMEM((3, 64, slots), f32),
            pltpu.VMEM((96, 2 * SIDE), bf16),
            pltpu.VMEM((2, 2, 48, SIDE), f32),
            pltpu.VMEM((2, 2, 48, SIDE), f32),
            pltpu.SemaphoreType.DMA((2, 2)),
            pltpu.SemaphoreType.DMA((2, 2)),
        ],
        compiler_params=pltpu.CompilerParams(
            collective_id=0, has_side_effects=True, vmem_limit_bytes=60 * 1024 * 1024
        ),
    )(
        adjoint_state, forward_velocity, density, lame_lambda, shear_modulus, neighbour, send_list,
        stage_a, deriv3, lift2, extract,
    )
    part = lax.psum_scatter(terms.reshape(3, -1), "event", scatter_dimension=1, tiled=True)
    return (velocity, part.reshape(3, 1, -1))


def solution(mesh):
    placed = (
        P("event", None, None, "dom"),
        P("event", None, None, None, "dom"),
        P(None, "dom"),
        P(None, "dom"),
        P(None, "dom"),
        P(None, "dom"),
        P(None, "dom"),
    )
    return jax.shard_map(
        local,
        mesh=mesh,
        in_specs=placed,
        out_specs=(P("event", None, None, "dom"), P(None, "dom", "event")),
        check_vma=False,
    )
```

time: 651 us -> 571 us (0.88); the launches traced: 641 us -> 571 us
  waiting for transfers between devices: 232 us -> 484 us
  local copies, waits for them, and re-layouts: 228 us -> 16.3 us
  other arithmetic: 76 us -> 0 us
  Pallas kernels: 0 us -> 56.7 us
  matrix products: 48.5 us -> 0 us
  starting transfers between devices: 40.4 us -> 0.04 us
    unnamed x1 -> x2, waiting for transfers between devices: 0.02 us -> 484 us
    psum x1 -> x0, waiting for transfers between devices: 232 us -> none  [local(): kernel_whole = kernel_whole + lax.psum(step_terms, 'event')]
    gather x35 -> x0, local copies, waits for them, and re-layouts: 98.3 us -> none  [the longest x6 55.6 us: partner_faces(): return jnp.take(combined, partner, axis=1).reshape(shape)]
    pallas_call x0 -> x1, Pallas kernels: none -> 56.7 us  [local(): pl.pallas_call(sim_kernel, out_shape=(jax.ShapeDtypeStruct((1, 3, 64, slo...]
    dot_general x15 -> x0, matrix products: 48.5 us -> none  [the longest x9 31.4 us: volume_grad(): jnp.einsum('an,cne->cae', deriv_stack, nodal_field, precision=lax.Precisi...]
    ppermute x12 -> x0, starting transfers between devices: 40.4 us -> none  [the longest x6 28.6 us: with_halo(): lax.ppermute(lax.slice_in_dim(block, 0, width, axis=dim), axis, backward)]
    reshape x17 -> x0, local copies, waits for them, and re-layouts: 30.6 us -> none  [the longest x9 16.8 us: partner_faces(): return jnp.take(combined, partner, axis=1).reshape(shape)]
    another operation x39 -> x0, local copies, waits for them, and re-layouts: 28.6 us -> none  [the longest x18 18 us: traction_of(): jnp.stack([traces[symmetric_index[component][0]] * shaped[0] + traces[sym...]
  transfers between devices with their start and end apart: 13 -> 1, of which waited for: 1 -> 1; matrix products, arithmetic and copies ran while one was open for 8% -> 0% of each run, Pallas kernels for 0% -> 0%
where the time goes in v1:
time: 571 us
  waiting for transfers between devices  484 us (85%)
  Pallas kernels  56.7 us (10%)
  local copies, waits for them, and re-layouts  16.3 us (3%)
  between operations  14 us (2%)
    unnamed x2, waiting for transfers between devices  484 us
    pallas_call x1, Pallas kernels, local(): pl.pallas_call(sim_kernel, out_shape=(jax.ShapeDtypeStruct((1, 3, 64, slo...  56.7 us
    unnamed x5, local copies, waits for them, and re-layouts  16.3 us
  transfers between devices with their start and end apart: 1, of which 1 were waited for; matrix products, arithmetic and copies ran while one was open for 0% of the time, Pallas kernels for 0%

profile of v1, /device:TPU:8, one launch (start us, length us, event | category | flops | bytes accessed | tf_op | source)
XLA Modules:
  0.0 570.7 jit_solution(10808992124369604308)
XLA Ops:
  7.2 0.0 reduce-scatter.4.cloned.1.call-start
  7.2 56.7 %shard_map.122 = (f32[1,3,64,768]{3,2,1,0:T(8,128)}, f32[3,64,768]{2,1,0:T(8,128)}) custom-call(f32[1,9,64,768]{3,2,1,0:T(8,128)} %state.1, f32[1,3,3,64,768]{4,3,2,1,0:T(8,128)} %forward.1, f32[64,768]{1,0:T(8,128)} %rho.1, f32[64,768]{1,0:T(8,128)} %lam.1, f32[64,768]{1,0:T(8,128)} %mu.1, s32[6,768]{1,0:T(8,128)} %near.1, s32[2,440]{1,0:T(2,128)} %sends.1, ...), custom_call_target="tpu_custom_call" | custom-call | tf_op jit(solution)/shard_map/pallas_call | solution.py:321
  63.9 13.6 %copy.16 = f32[3,64,768]{0,2,1:T(8,128)} copy(f32[3,64,768]{2,1,0:T(8,128)} %get-tuple-element.5) | data formatting | bytes 1179648
  77.6 0.0 copy-start
  77.6 0.0 reduce-scatter.4.cloned.1.call-update
  77.6 483.6 %reduce-scatter.4.cloned.1.call-done = f32[1024,3]{1,0:T(8,128)} async-done(((f32[49152,3]{1,0:T(8,128)}), f32[1024,3]{1,0:T(8,128)}) %reduce-scatter.4.cloned.1.call-update) | async-done | bytes 12304
  561.2 1.8 copy.13
  563.0 0.0 copy-done
  563.0 0.8 copy.20
Async XLA Ops:
  7.2 554.0 %reduce-scatter.4.cloned.1.call-start = ((), (), s32[]{:S(2)}) async-start(), calls=%async_computation.1 | async-start | bytes 25690112
  77.6 485.5 %copy-start = (f32[1,3,64,768]{3,2,1,0:T(8,128)S(1)}, f32[1,3,64,768]{3,2,1,0:T(8,128)}, u32[]{:S(2)}) copy-start(f32[1,3,64,768]{3,2,1,0:T(8,128)} %get-tuple-element.10) | copy-start | bytes 1769476
Sparse Core Ops, SparseCore 0:
  77.7 483.4 reduce-scatter.3

commit v2 on v1

--- a/solution.py
+++ b/solution.py
@@ -14,6 +14,7 @@
 half_lift = 3.0
 symmetric_index = ((0, 3, 4), (3, 1, 5), (4, 5, 2))
 SIDE = 512
+NX, NZ = 4, 12
 MESH = pl.DeviceIdType.MESH
 f32 = jnp.float32
 bf16 = jnp.bfloat16
@@ -108,9 +109,10 @@
 
 def sim_kernel(
     state, forward, rho, lam, mu, near, sends, stage_a, deriv3, lift2, extract,
-    vel, acc,
-    sig, onehot, pick, send_ids, traces, jump, grad_in, grad, fgrad, sig_in, jump_in, impulse, div,
-    halves, out_buf, in_buf, send_sem, recv_sem,
+    vel, part,
+    acc, sig, onehot, pick, send_ids, traces, jump, grad_in, grad, fgrad, sig_in, jump_in, impulse, div,
+    halves, out_buf, in_buf, x_in, x_sum, z_out, z_in,
+    send_sem, recv_sem, x_send, x_recv, z_send, z_recv,
 ):
     count = lax.axis_size("dom")
     me = lax.axis_index("dom")
@@ -124,6 +126,66 @@
     barrier = pltpu.get_barrier_semaphore()
     for other in (lower, upper):
         pl.semaphore_signal(barrier, inc=1, device_id={"dom": other}, device_id_type=MESH)
+    event = lax.axis_index("event")
+    along_x, along_z = event // NZ, lax.rem(event, NZ)
+    x_peers = [lax.rem(along_x + d, NX) for d in range(1, NX)]
+    z_peers = [lax.rem(along_z + d, NZ) for d in range(1, NZ)]
+    peers = [p * NZ + along_z for p in x_peers] + [along_x * NZ + p for p in z_peers]
+    for other in peers:
+        pl.semaphore_signal(barrier, inc=1, device_id={"event": other}, device_id_type=MESH)
+    band = 64 // NX
+
+    def x_copies(group):
+        terms = slice(1, 3) if group == 0 else slice(0, 1)
+        return [
+            pltpu.make_async_remote_copy(
+                src_ref=acc.at[terms, pl.ds(pl.multiple_of(p * band, band), band), :],
+                dst_ref=x_in.at[d, terms],
+                send_sem=x_send.at[group, d],
+                recv_sem=x_recv.at[group, d],
+                device_id={"event": p * NZ + along_z},
+                device_id_type=MESH,
+            )
+            for d, p in enumerate(x_peers)
+        ]
+
+    def z_copies(group):
+        terms = slice(1, 3) if group == 0 else slice(0, 1)
+        return [
+            pltpu.make_async_remote_copy(
+                src_ref=z_out.at[p, terms],
+                dst_ref=z_in.at[d, terms],
+                send_sem=z_send.at[group, d],
+                recv_sem=z_recv.at[group, d],
+                device_id={"event": along_x * NZ + p},
+                device_id_type=MESH,
+            )
+            for d, p in enumerate(z_peers)
+        ]
+
+    def scatter_on(group):
+        for copy in x_copies(group):
+            copy.wait()
+        mine = pl.ds(pl.multiple_of(along_x * band, band), band)
+        for t in (1, 2) if group == 0 else (0,):
+            total = acc[t, mine, :]
+            for d in range(NX - 1):
+                total = total + x_in[d, t]
+            x_sum[t] = total
+            for piece in range(band * slots // 128):
+                row, column = piece // (slots // 128), piece % (slots // 128) * 128
+                z_out[piece // 8, t, piece % 8 : piece % 8 + 1, :] = x_sum[t, row : row + 1, column : column + 128]
+        for copy in z_copies(group):
+            copy.start()
+
+    def gather_in(group):
+        for copy in z_copies(group):
+            copy.wait()
+        for t in (1, 2) if group == 0 else (0,):
+            total = z_out[along_z, t]
+            for d in range(NZ - 1):
+                total = total + z_in[d, t]
+            part[t] = total
 
     valid = jnp.where(jnp.max(near[...], axis=0, keepdims=True) >= 0, 1.0, 0.0)
     for c in range(3):
@@ -248,7 +310,7 @@
 
         @pl.when(n == 0)
         def _():
-            pl.semaphore_wait(barrier, 2)
+            pl.semaphore_wait(barrier, 2 + len(peers))
 
         send(0)
 
@@ -292,6 +354,12 @@
             contraction = contraction + (g[0][2] + g[2][0]) * s[4]
             contraction = contraction + (g[1][2] + g[2][1]) * s[5]
             acc[2, rows] = acc[2, rows] - (2.0 * time_step) * contraction
+
+        @pl.when(n == steps - 1)
+        def _():
+            for copy in x_copies(0):
+                copy.start()
+
         arrive(1, jump_in, 0)
         for c in range(3):
             impulse[c] = dot(lift2[...], jump_in[c])
@@ -309,6 +377,12 @@
         return carry
 
     lax.fori_loop(0, steps, step, 0)
+    for copy in x_copies(1):
+        copy.start()
+    scatter_on(0)
+    scatter_on(1)
+    gather_in(0)
+    gather_in(1)
 
 
 def local(
@@ -318,15 +392,17 @@
     top = slots + 2 * SIDE
     stage_a, deriv3, lift2, extract = (jnp.asarray(x) for x in tables())
     vmem = pl.BlockSpec(memory_space=pltpu.VMEM)
-    velocity, terms = pl.pallas_call(
+    share = 64 * slots // (NX * NZ)
+    velocity, part = pl.pallas_call(
         sim_kernel,
         out_shape=(
             jax.ShapeDtypeStruct((1, 3, 64, slots), f32),
-            jax.ShapeDtypeStruct((3, 64, slots), f32),
+            jax.ShapeDtypeStruct((3, share // 128, 128), f32),
         ),
         in_specs=[vmem] * 11,
         out_specs=(vmem, vmem),
         scratch_shapes=[
+            pltpu.VMEM((3, 64, slots), f32),
             pltpu.VMEM((6, 64, slots), f32),
             pltpu.VMEM((6, top, slots), bf16),
             pltpu.VMEM((slots, 2 * SIDE), bf16),
@@ -343,8 +419,16 @@
             pltpu.VMEM((96, 2 * SIDE), bf16),
             pltpu.VMEM((2, 2, 48, SIDE), f32),
             pltpu.VMEM((2, 2, 48, SIDE), f32),
+            pltpu.VMEM((NX - 1, 3, 64 // NX, slots), f32),
+            pltpu.VMEM((3, 64 // NX, slots), f32),
+            pltpu.VMEM((NZ, 3, share // 128, 128), f32),
+            pltpu.VMEM((NZ - 1, 3, share // 128, 128), f32),
             pltpu.SemaphoreType.DMA((2, 2)),
             pltpu.SemaphoreType.DMA((2, 2)),
+            pltpu.SemaphoreType.DMA((2, NX - 1)),
+            pltpu.SemaphoreType.DMA((2, NX - 1)),
+            pltpu.SemaphoreType.DMA((2, NZ - 1)),
+            pltpu.SemaphoreType.DMA((2, NZ - 1)),
         ],
         compiler_params=pltpu.CompilerParams(
             collective_id=0, has_side_effects=True, vmem_limit_bytes=60 * 1024 * 1024
@@ -353,7 +437,6 @@
         adjoint_state, forward_velocity, density, lame_lambda, shear_modulus, neighbour, send_list,
         stage_a, deriv3, lift2, extract,
     )
-    part = lax.psum_scatter(terms.reshape(3, -1), "event", scatter_dimension=1, tiled=True)
     return (velocity, part.reshape(3, 1, -1))
 
 

time: 571 us -> 81.6 us (0.14)
  the two profiles are of different devices: /device:TPU:8 before, /device:TPU:25 now
where the time goes in v2:
time: 81.6 us; the launch traced here: 81.3 us
  Pallas kernels  77.5 us (95%)
  local copies, waits for them, and re-layouts  3.22 us (4%)
    pallas_call x1, Pallas kernels, local(): pl.pallas_call(sim_kernel, out_shape=(jax.ShapeDtypeStruct((1, 3, 64, slo...  77.5 us
    unnamed x2, local copies, waits for them, and re-layouts  3.22 us

profile of v2, /device:TPU:25, one launch (start us, length us, event | category | flops | bytes accessed | tf_op | source)
XLA Modules:
  0.0 81.3 jit_solution(14000543817353808330)
XLA Ops:
  0.6 77.5 %shard_map.122 = (f32[1,3,64,768]{3,2,1,0:T(8,128)}, f32[3,8,128]{2,1,0:T(8,128)}) custom-call(f32[1,9,64,768]{3,2,1,0:T(8,128)} %state.1, f32[1,3,3,64,768]{4,3,2,1,0:T(8,128)} %forward.1, f32[64,768]{1,0:T(8,128)} %rho.1, f32[64,768]{1,0:T(8,128)} %lam.1, f32[64,768]{1,0:T(8,128)} %mu.1, s32[6,768]{1,0:T(8,128)} %near.1, s32[2,440]{1,0:T(2,128)} %sends.1, ...), custom_call_target="tpu_custom_call" | custom-call | tf_op jit(solution)/shard_map/pallas_call | solution.py:396
  78.1 1.9 %copy.17 = f32[1,3,64,768]{3,2,1,0:T(8,128)} copy(f32[1,3,64,768]{3,2,1,0:T(8,128)} %get-tuple-element.12) | data formatting | bytes 1179648
  80.0 1.3 %copy.18 = f32[3,1,1024]{2,1,0:T(1,128)} copy(f32[3,1,1024]{2,1,0:T(1,128)} %bitcast.1) | data formatting | bytes 24576

commit v3 on v2

v3 whole, which is shorter than its diff:
```python
import functools
import math

import jax
import jax.numpy as jnp
import numpy as np
from jax import lax
from jax.experimental import pallas as pl
from jax.experimental.pallas import tpu as pltpu
from jax.sharding import PartitionSpec as P
import ml_dtypes

time_step = 0.02
half_lift = 3.0
symmetric_index = ((0, 3, 4), (3, 1, 5), (4, 5, 2))
SIDE = 512
HALF = 384
NX, NZ = 4, 12
SUM_EVENTS = True
MESH = pl.DeviceIdType.MESH
f32 = jnp.float32
bf16 = jnp.bfloat16


def lobatto_diff():
    points = [-1.0, -1.0 / math.sqrt(5.0), 1.0 / math.sqrt(5.0), 1.0]
    weights = [
        1.0 / math.prod([points[target] - points[other] for other in range(4) if other != target])
        for target in range(4)
    ]
    offdiag = [
        [
            (
                0.0
                if target == source
                else weights[source] / weights[target] / (points[target] - points[source])
            )
            for source in range(4)
        ]
        for target in range(4)
    ]
    return np.array(
        [
            [
                -sum(offdiag[target]) if target == source else offdiag[target][source]
                for source in range(4)
            ]
            for target in range(4)
        ],
        dtype=np.float32,
    )


def deriv_table():
    matrix = lobatto_diff()
    identity = np.eye(4, dtype=np.float32)
    return np.concatenate(
        [
            np.kron(np.kron(matrix, identity), identity),
            np.kron(np.kron(identity, matrix), identity),
            np.kron(np.kron(identity, identity), matrix),
        ],
        axis=0,
    ).astype(np.float32)


def face_nodes():
    nodes = np.zeros((6, 16), np.int32)
    for face in range(6):
        for q in range(16):
            coordinates = [q // 4, q % 4]
            coordinates.insert(face // 2, 3 * (face % 2))
            nodes[face, q] = 16 * coordinates[0] + 4 * coordinates[1] + coordinates[2]
    return nodes


def tables():
    to_bf16 = lambda x: np.asarray(x, np.float32).astype(ml_dtypes.bfloat16)
    deriv = deriv_table()
    high = to_bf16(deriv)
    low = to_bf16(deriv - high.astype(np.float32))
    deriv3 = np.concatenate([high, low, high], axis=1)
    nodes = face_nodes()
    signed = np.zeros((192, 96), np.float32)
    summed = np.zeros((64, 96), np.float32)
    plain = np.zeros((64, 96), np.float32)
    for face in range(6):
        sign = face % 2 * 2 - 1.0
        for q in range(16):
            column, node = face * 16 + q, nodes[face, q]
            signed[face // 2 * 64 + node, column] = half_lift * sign
            summed[node, column] = half_lift * sign
            plain[node, column] = half_lift
    stage_j = np.concatenate([signed, plain], axis=0)
    stage_j = np.concatenate([stage_j, stage_j], axis=1)
    lift2 = np.concatenate([summed, summed], axis=1)
    return deriv3, to_bf16(stage_j), to_bf16(lift2)


def split(x):
    high = x.astype(bf16)
    return high, (x - high.astype(f32)).astype(bf16)


def face_rows(tiles, dim):
    if dim == 0:
        return tiles[0:2], tiles[6:8]
    sub = lax.broadcasted_iota(jnp.int32, tiles[0].shape, 0)
    roll = lambda x, by: pltpu.roll(x, by % 8, 0) if by % 8 else x
    if dim == 1:
        low = [jnp.where(sub < 4, tiles[k], roll(tiles[k + 2], 4)) for k in (0, 4)]
        high = [jnp.where(sub < 4, roll(tiles[k + 1], 4), tiles[k + 3]) for k in (0, 4)]
        return low, high
    out = []
    for start in (0, 3):
        rows = []
        for k in (0, 4):
            total = roll(tiles[k], -start)
            for q in range(1, 8):
                total = jnp.where(sub == q, roll(tiles[k + q // 2], q - start - q % 2 * 4), total)
            rows.append(total)
        out.append(rows)
    return out


def dot(a, b):
    return jnp.dot(a, b, preferred_element_type=f32)


def sim_kernel(
    state, forward_hbm, rho, lam, mu, near, sends, stage_v, stage_j, lift2,
    vel_hbm, part,
    vel, forward, acc, sig, onehot, pick, spread, own_tile, own_hit, side_tile, side_hit, send_ids,
    traces, jump, field_in, jump_in, grad, kick, fgrad, sig_in, impulse, div, halves, face_at,
    out_buf, in_buf, x_in, x_sum, z_out, z_in,
    load_sem, send_sem, recv_sem, x_send, x_recv, z_send, z_recv,
):
    count = lax.axis_size("dom")
    me = lax.axis_index("dom")
    lower = lax.rem(me + count - 1, count)
    upper = lax.rem(me + 1, count)
    slots = rho.shape[1]
    cap = sends.shape[1]
    steps = forward.shape[0]

    load_v = pltpu.make_async_copy(state.at[0, 0:3], vel, load_sem.at[0])
    load_s = pltpu.make_async_copy(state.at[0, 3:9], sig, load_sem.at[1])
    load_f = pltpu.make_async_copy(forward_hbm.at[0], forward, load_sem.at[2])
    load_v.start()
    load_s.start()
    load_f.start()

    barrier = pltpu.get_barrier_semaphore()
    for other in (lower, upper):
        pl.semaphore_signal(barrier, inc=1, device_id={"dom": other}, device_id_type=MESH)
    event = lax.axis_index("event")
    along_x, along_z = event // NZ, lax.rem(event, NZ)
    x_peers = [lax.rem(along_x + d, NX) for d in range(1, NX)]
    z_peers = [lax.rem(along_z + d, NZ) for d in range(1, NZ)]
    peers = [p * NZ + along_z for p in x_peers] + [along_x * NZ + p for p in z_peers]
    if not SUM_EVENTS:
        peers = []
    for other in peers:
        pl.semaphore_signal(barrier, inc=1, device_id={"event": other}, device_id_type=MESH)
    band = 64 // NX

    def x_copies(group):
        terms = slice(1, 3) if group == 0 else slice(0, 1)
        return [
            pltpu.make_async_remote_copy(
                src_ref=acc.at[terms, pl.ds(pl.multiple_of(p * band, band), band), :],
                dst_ref=x_in.at[d, terms],
                send_sem=x_send.at[group, d],
                recv_sem=x_recv.at[group, d],
                device_id={"event": p * NZ + along_z},
                device_id_type=MESH,
            )
            for d, p in enumerate(x_peers)
        ]

    def z_copies(group):
        terms = slice(1, 3) if group == 0 else slice(0, 1)
        return [
            pltpu.make_async_remote_copy(
                src_ref=z_out.at[p, terms],
                dst_ref=z_in.at[d, terms],
                send_sem=z_send.at[group, d],
                recv_sem=z_recv.at[group, d],
                device_id={"event": along_x * NZ + p},
                device_id_type=MESH,
            )
            for d, p in enumerate(z_peers)
        ]

    def scatter_on(group):
        for copy in x_copies(group):
            copy.wait()
        mine = pl.ds(pl.multiple_of(along_x * band, band), band)
        for t in (1, 2) if group == 0 else (0,):
            total = acc[t, mine, :]
            for d in range(NX - 1):
                total = total + x_in[d, t]
            x_sum[t] = total
            for piece in range(band * slots // 128):
                row, column = piece // (slots // 128), piece % (slots // 128) * 128
                z_out[piece // 8, t, piece % 8 : piece % 8 + 1, :] = x_sum[t, row : row + 1, column : column + 128]
        for copy in z_copies(group):
            copy.start()

    def gather_in(group):
        for copy in z_copies(group):
            copy.wait()
        for t in (1, 2) if group == 0 else (0,):
            total = z_out[along_z, t]
            for d in range(NZ - 1):
                total = total + z_in[d, t]
            for row in range(8):
                part[t, :, row * 128 : row * 128 + 128] = total[row : row + 1, :]

    acc[...] = jnp.zeros_like(acc)

    send_ids[...] = jnp.full_like(send_ids, -1)
    send_ids[0:1, 0:cap] = sends[0:1, :]
    send_ids[0:1, SIDE : SIDE + cap] = sends[1:2, :]
    ids = send_ids[0:1, :]
    face_of = jnp.where(ids < 0, -1, 0)
    for f in range(1, 6):
        face_of = face_of + jnp.where(ids >= f * slots, 1, 0)
    slot_of = jnp.where(ids < 0, -1, ids - face_of * slots)

    def tile_of(index):
        width = index.shape[1]
        tile = jnp.right_shift(index, 4)
        row = lax.broadcasted_iota(jnp.int32, (16, width), 0)
        hit = jnp.where(jnp.bitwise_and(index, 15) == row, 1.0, 0.0)
        return jnp.broadcast_to(tile.astype(f32), (16, width)).astype(bf16), hit.astype(bf16)

    spread[0], spread[1] = tile_of(slot_of)

    def build_pick(k, carry):
        rows = pl.ds(pl.multiple_of(k * 16, 16), 16)
        level = jnp.full((16, 2 * SIDE), k.astype(f32)).astype(bf16)
        pick[rows, :] = jnp.where(spread[0] == level, spread[1], jnp.zeros_like(level))
        return carry

    lax.fori_loop(0, slots // 16, build_pick, 0)

    def build_onehot():
        for f in range(6):
            code = near[f : f + 1, :]
            own_tile[f], own_hit[f] = tile_of(code)
            at = jnp.where(code >= slots + cap, code - (slots + cap - SIDE), code - slots)
            side_tile[f], side_hit[f] = tile_of(jnp.where(code >= slots, at, -1))

        def body(k, carry):
            rows = pl.ds(pl.multiple_of(k * 16, 16), 16)
            level = jnp.full((16, slots), k.astype(f32)).astype(bf16)
            for f in range(6):
                onehot[f, rows, :] = jnp.where(own_tile[f] == level, own_hit[f], jnp.zeros_like(level))
            return carry

        lax.fori_loop(0, slots // 16, body, 0)

        def side_body(k, carry):
            rows = pl.ds(pl.multiple_of(k * 16, 16), 16)
            level = jnp.full((16, slots), k.astype(f32)).astype(bf16)
            total = jnp.zeros_like(level)
            for f in range(6):
                total = total + jnp.where(side_tile[f] == level, side_hit[f] * (f + 1.0), jnp.zeros_like(level))
            onehot[6, pl.ds(pl.multiple_of(k * 16, 16), 16), :] = total
            return carry

        lax.fori_loop(0, 2 * SIDE // 16, side_body, 0)
        ones = jnp.ones((16, slots), bf16)
        face_at[...] = lax.dot_general(
            ones, onehot[6], (((1,), (1,)), ((), ())), preferred_element_type=f32
        )

        def side_ones(k, carry):
            rows = pl.ds(pl.multiple_of(k * 16, 16), 16)
            onehot[6, rows, :] = jnp.minimum(onehot[6, rows, :], jnp.ones((16, slots), bf16))
            return carry

        lax.fori_loop(0, 2 * SIDE // 16, side_ones, 0)

    def inner_of(f):
        return jnp.where(near[f : f + 1, :] >= 0, 1.0, 0.0)

    def copy_out(phase, side, piece):
        other = upper if side else lower
        return pltpu.make_async_remote_copy(
            src_ref=out_buf.at[phase, side, piece],
            dst_ref=in_buf.at[phase, 1 - side, piece],
            send_sem=send_sem.at[phase, side, piece],
            recv_sem=recv_sem.at[phase, 1 - side, piece],
            device_id={"dom": other},
            device_id_type=MESH,
        )

    pieces = [(side, piece) for piece in range(SIDE // 256) for side in range(2)]

    def send(phase):
        rows = traces[...].reshape(576, slots)
        for number, (side, piece) in enumerate(pieces):
            start = side * SIDE + piece * 256
            got = dot(rows, pick[:, start : start + 256])
            face = face_of[:, start : start + 256]
            total = jnp.zeros((48, 256), f32)
            for f in range(6):
                both = got[f * 96 : f * 96 + 48] + got[f * 96 + 48 : f * 96 + 96]
                total = jnp.where(face == f, both, total)
            out_buf[phase, side, piece] = total
            if number % 2:
                for end in range(2):
                    copy_out(phase, end, piece).start()

    def own(phase):
        for f in range(6):
            got = dot(traces[f ^ 1], onehot[f, 0:slots, :])
            mine = traces[f, 0:48].astype(f32) + traces[f, 48:96].astype(f32)
            weight = inner_of(f) if phase == 0 else 2.0 - inner_of(f)
            jump[f] = got[0:48] + got[48:96] - mine * weight

    def arrive(phase):
        for side, piece in pieces:
            copy_out(phase, side, piece).wait()
        for side, piece in pieces:
            start = side * SIDE + piece * 256
            columns = slice(start, start + 256)
            high, low = split(in_buf[phase, side, piece])
            for f in range(6):
                chosen = jnp.broadcast_to(
                    jnp.where(face_at[0:1, columns] == f + 1.0, 1.0, 0.0), (16, 256)
                ).astype(bf16)
                for c in range(3):
                    rows = slice(c * 16, c * 16 + 16)
                    halves[f * 96 + c * 16 : f * 96 + c * 16 + 16, columns] = high[rows] * chosen
                    halves[f * 96 + 48 + c * 16 : f * 96 + 64 + c * 16, columns] = low[rows] * chosen
        for t in range(0, slots, 256):
            columns = slice(t, t + 256)
            got = dot(halves[...], onehot[6, :, columns])
            for f in range(6):
                total = jump[f, :, columns] + got[f * 96 : f * 96 + 48] + got[f * 96 + 48 : f * 96 + 96]
                high, low = split(total)
                for c in range(3):
                    jump_in[c, f * 16 : f * 16 + 16, columns] = high[c * 16 : c * 16 + 16]
                    jump_in[c, 96 + f * 16 : 112 + f * 16, columns] = low[c * 16 : c * 16 + 16]

    def put3(ref, index, high, low):
        ref[index, 0:64] = high
        ref[index, 64:128] = high
        ref[index, 128:192] = low

    def put_traces(field, pairs):
        for h in range(0, slots, HALF):
            columns = slice(h, h + HALF)
            tiles = [field[k * 8 : k * 8 + 8, columns] for k in range(8)]
            for c, d in pairs:
                for end, rows in enumerate(face_rows(tiles, d)):
                    high, low = split(jnp.concatenate(rows, axis=0))
                    traces[2 * d + end, c * 16 : c * 16 + 16, columns] = high
                    traces[2 * d + end, 48 + c * 16 : 64 + c * 16, columns] = low

    def velocity_traces():
        for c in range(3):
            put_traces(vel.at[c], [(c, d) for d in range(3)])

    def stress_traces():
        for m, pairs in enumerate(
            (((0, 0),), ((1, 1),), ((2, 2),), ((1, 0), (0, 1)), ((2, 0), (0, 2)), ((2, 1), (1, 2)))
        ):
            put_traces(sig.at[m], pairs)

    blocks = [
        (r, slice(r, r + 8), slice(h, h + HALF)) for r in range(0, 64, 8) for h in range(0, slots, HALF)
    ]

    def step(n, carry):
        velocity_traces()

        @pl.when(n == 0)
        def _():
            pl.semaphore_wait(barrier, 2 + len(peers))

        send(0)

        @pl.when(n == 0)
        def _():
            build_onehot()
            load_s.wait()
            for c in range(6):
                sig[c] = sig[c] * valid
            load_f.wait()

        own(0)
        for c in range(3):
            high, low = split(vel[c])
            put3(field_in, c, high, low)
        for c in range(3):
            high, low = split(forward[n, c])
            fgrad[c] = dot(stage_v[...], jnp.concatenate([high, high, low], axis=0))
            grad[c] = dot(stage_v[...], field_in[c])
        arrive(0)
        for c in range(3):
            got = dot(stage_j[...], jump_in[c])
            impulse[c] = got[0:192]
            kick[c] = got[192:256]
        for r, rows, cols in blocks:
            g = [
                [
                    grad[i, j * 64 + r : j * 64 + r + 8, cols] + impulse[i, j * 64 + r : j * 64 + r + 8, cols]
                    for j in range(3)
                ]
                for i in range(3)
            ]
            shear = mu[rows, cols] * time_step
            bulk = lam[rows, cols] * time_step * (g[0][0] + g[1][1] + g[2][2])
            for c in range(3):
                sig[c, rows, cols] = sig[c, rows, cols] + (bulk + 2.0 * shear * g[c][c])
            for m, (i, j) in ((3, (0, 1)), (4, (0, 2)), (5, (1, 2))):
                sig[m, rows, cols] = sig[m, rows, cols] + shear * (g[i][j] + g[j][i])
        stress_traces()
        send(1)
        for r, rows, cols in blocks:
            g = [[fgrad[i, j * 64 + r : j * 64 + r + 8, cols] for j in range(3)] for i in range(3)]
            s = [sig[m, rows, cols] for m in range(6)]
            rate = g[0][0] + g[1][1] + g[2][2]
            acc[1, rows, cols] = acc[1, rows, cols] - time_step * rate * (s[0] + s[1] + s[2])
            contraction = g[0][0] * s[0] + g[1][1] * s[1] + g[2][2] * s[2]
            contraction = contraction + (g[0][1] + g[1][0]) * s[3]
            contraction = contraction + (g[0][2] + g[2][0]) * s[4]
            contraction = contraction + (g[1][2] + g[2][1]) * s[5]
            acc[2, rows, cols] = acc[2, rows, cols] - (2.0 * time_step) * contraction

        if SUM_EVENTS:
            @pl.when(n == steps - 1)
            def _():
                for copy in x_copies(0):
                    copy.start()

        own(1)
        for m in range(6):
            high, low = split(sig[m])
            put3(sig_in, m, high, low)
        for c in range(3):
            total = dot(stage_v[0:64], sig_in[symmetric_index[c][0]])
            total = total + dot(stage_v[64:128], sig_in[symmetric_index[c][1]])
            total = total + dot(stage_v[128:192], sig_in[symmetric_index[c][2]])
            div[c] = total
        arrive(1)
        for c in range(3):
            impulse[c, 0:64] = dot(lift2[...], jump_in[c])
        for r, rows, cols in blocks:
            z = jnp.sqrt(rho[rows, cols] * (lam[rows, cols] + 2.0 * mu[rows, cols]))
            scale = time_step / rho[rows, cols]
            total = jnp.zeros_like(z)
            for c in range(3):
                rate = div[c, rows, cols] + impulse[c, rows, cols] + z * kick[c, rows, cols]
                new = vel[c, rows, cols] + scale * rate
                vel[c, rows, cols] = new
                total = total + forward[n, c, rows, cols] * new
            acc[0, rows, cols] = acc[0, rows, cols] - time_step * total
        return carry

    valid = jnp.where(jnp.max(near[...], axis=0, keepdims=True) >= 0, 1.0, 0.0)
    load_v.wait()
    for c in range(3):
        vel[c] = vel[c] * valid
    lax.fori_loop(0, steps, step, 0)
    store_v = pltpu.make_async_copy(vel, vel_hbm.at[0], load_sem.at[0])
    if SUM_EVENTS:
        for copy in x_copies(1):
            copy.start()
    store_v.start()
    if SUM_EVENTS:
        scatter_on(0)
        scatter_on(1)
        gather_in(0)
        gather_in(1)
    else:
        part[...] = acc[...]
    store_v.wait()


def hand_out(vel_in, part_in, vel_out, part_out, vel, part, sem):
    loads = [pltpu.make_async_copy(vel_in, vel, sem.at[0]), pltpu.make_async_copy(part_in, part, sem.at[1])]
    stores = [pltpu.make_async_copy(vel, vel_out, sem.at[2]), pltpu.make_async_copy(part, part_out, sem.at[3])]
    for copy in loads:
        copy.start()
    for load, store in zip(loads, stores):
        load.wait()
        store.start()
    for copy in stores:
        copy.wait()


def local(
    adjoint_state, forward_velocity, density, lame_lambda, shear_modulus, neighbour, send_list
):
    slots = density.shape[1]
    stage_v, stage_j, lift2 = (jnp.asarray(x) for x in tables())
    vmem = pl.BlockSpec(memory_space=pltpu.VMEM)
    hbm = pl.BlockSpec(memory_space=pl.ANY)
    share = 64 * slots // (NX * NZ)
    steps = forward_velocity.shape[1]
    velocity, part = pl.pallas_call(
        sim_kernel,
        out_shape=(
            jax.ShapeDtypeStruct((1, 3, 64, slots), f32),
            jax.ShapeDtypeStruct((3, 1, share) if SUM_EVENTS else (3, 64, slots), f32),
        ),
        in_specs=[hbm] * 2 + [vmem] * 8,
        out_specs=(hbm, vmem),
        scratch_shapes=[
            pltpu.VMEM((3, 64, slots), f32),
            pltpu.VMEM((steps, 3, 64, slots), f32),
            pltpu.VMEM((3, 64, slots), f32),
            pltpu.VMEM((6, 64, slots), f32),
            pltpu.VMEM((7, 2 * SIDE, slots), bf16),
            pltpu.VMEM((slots, 2 * SIDE), bf16),
            pltpu.VMEM((2, 16, 2 * SIDE), bf16),
            pltpu.VMEM((6, 16, slots), bf16),
            pltpu.VMEM((6, 16, slots), bf16),
            pltpu.VMEM((6, 16, slots), bf16),
            pltpu.VMEM((6, 16, slots), bf16),
            pltpu.VMEM((8, 2 * SIDE), jnp.int32),
            pltpu.VMEM((6, 96, slots), bf16),
            pltpu.VMEM((6, 48, slots), f32),
            pltpu.VMEM((3, 192, slots), bf16),
            pltpu.VMEM((3, 192, slots), bf16),
            pltpu.VMEM((3, 192, slots), f32),
            pltpu.VMEM((3, 64, slots), f32),
            pltpu.VMEM((3, 192, slots), f32),
            pltpu.VMEM((6, 192, slots), bf16),
            pltpu.VMEM((3, 192, slots), f32),
            pltpu.VMEM((3, 64, slots), f32),
            pltpu.VMEM((576, 2 * SIDE), bf16),
            pltpu.VMEM((16, 2 * SIDE), f32),
            pltpu.VMEM((2, 2, SIDE // 256, 48, 256), f32),
            pltpu.VMEM((2, 2, SIDE // 256, 48, 256), f32),
            pltpu.VMEM((NX - 1, 3, 64 // NX, slots), f32),
            pltpu.VMEM((3, 64 // NX, slots), f32),
            pltpu.VMEM((NZ, 3, share // 128, 128), f32),
            pltpu.VMEM((NZ - 1, 3, share // 128, 128), f32),
            pltpu.SemaphoreType.DMA((3,)),
            pltpu.SemaphoreType.DMA((2, 2, SIDE // 256)),
            pltpu.SemaphoreType.DMA((2, 2, SIDE // 256)),
            pltpu.SemaphoreType.DMA((2, NX - 1)),
            pltpu.SemaphoreType.DMA((2, NX - 1)),
            pltpu.SemaphoreType.DMA((2, NZ - 1)),
            pltpu.SemaphoreType.DMA((2, NZ - 1)),
        ],
        compiler_params=pltpu.CompilerParams(
            collective_id=0, has_side_effects=True, vmem_limit_bytes=60 * 1024 * 1024
        ),
    )(
        adjoint_state, forward_velocity, density, lame_lambda, shear_modulus, neighbour, send_list,
        stage_v, stage_j, lift2,
    )
    if not SUM_EVENTS:
        part = part.reshape(3, 1, -1)
    return pl.pallas_call(
        hand_out,
        out_shape=tuple(jax.ShapeDtypeStruct(x.shape, f32) for x in (velocity, part)),
        in_specs=[hbm, hbm],
        out_specs=(hbm, hbm),
        scratch_shapes=[
            pltpu.VMEM(velocity.shape, f32),
            pltpu.VMEM(part.shape, f32),
            pltpu.SemaphoreType.DMA((4,)),
        ],
    )(velocity, part)


def solution(mesh):
    placed = (
        P("event", None, None, "dom"),
        P("event", None, None, None, "dom"),
        P(None, "dom"),
        P(None, "dom"),
        P(None, "dom"),
        P(None, "dom"),
        P(None, "dom"),
    )
    return jax.shard_map(
        local,
        mesh=mesh,
        in_specs=placed,
        out_specs=(P("event", None, None, "dom"), P(None, "dom", "event")),
        check_vma=False,
    )
```

time: 81.6 us -> 73.6 us (0.902)
  Pallas kernels: 77.5 us -> 72.8 us
  local copies, waits for them, and re-layouts: 3.22 us -> 0 us
    pallas_call x1, Pallas kernels: 77.5 us -> 70.9 us  [local(): pl.pallas_call(sim_kernel, out_shape=(jax.ShapeDtypeStruct((1, 3, 64, slo...]
    unnamed x2 -> x0, local copies, waits for them, and re-layouts: 3.22 us -> none
    pallas_call x0 -> x1, Pallas kernels: none -> 1.92 us  [local(): pl.pallas_call(hand_out, out_shape=tuple((jax.ShapeDtypeStruct(x.shape, f...]
where the time goes in v3:
time: 73.6 us; the launch traced here: 73.5 us
  Pallas kernels  72.8 us (99%)
    pallas_call x1, Pallas kernels, local(): pl.pallas_call(sim_kernel, out_shape=(jax.ShapeDtypeStruct((1, 3, 64, slo...  70.9 us
    pallas_call x1, Pallas kernels, local(): pl.pallas_call(hand_out, out_shape=tuple((jax.ShapeDtypeStruct(x.shape, f...  1.92 us

profile of v3, /device:TPU:25, one launch (start us, length us, event | category | flops | bytes accessed | tf_op | source)
XLA Modules:
  0.0 73.5 jit_solution(116820518187084753)
XLA Ops:
  0.6 70.9 %shard_map.113 = (f32[1,3,64,768]{3,2,1,0:T(8,128)}, f32[3,1,1024]{2,1,0:T(1,128)}) custom-call(f32[1,9,64,768]{3,2,1,0:T(8,128)} %state.1, f32[1,3,3,64,768]{4,3,2,1,0:T(8,128)} %forward_hbm.1, f32[64,768]{1,0:T(8,128)} %rho.1, f32[64,768]{1,0:T(8,128)} %lam.1, f32[64,768]{1,0:T(8,128)} %mu.1, s32[6,768]{1,0:T(8,128)} %near.1, s32[2,440]{1,0:T(2,128)} %sends.1, ...), custom_call_target="tpu_custom_call" | custom-call | tf_op jit(solution)/shard_map/pallas_call | solution.py:506
  71.6 1.9 %shard_map.114 = (f32[1,3,64,768]{3,2,1,0:T(8,128)}, f32[3,1,1024]{2,1,0:T(1,128)}) custom-call(f32[1,3,64,768]{3,2,1,0:T(8,128)} %get-tuple-element.4.vel_in, f32[3,1,1024]{2,1,0:T(1,128)} %get-tuple-element.5.part_in), custom_call_target="tpu_custom_call" | custom-call | tf_op jit(solution)/shard_map/pallas_call | solution.py:562

commit v4 on v3

--- a/solution.py
+++ b/solution.py
@@ -131,7 +131,7 @@
     state, forward_hbm, rho, lam, mu, near, sends, stage_v, stage_j, lift2,
     vel_hbm, part,
     vel, forward, acc, sig, onehot, pick, spread, own_tile, own_hit, side_tile, side_hit, send_ids,
-    traces, jump, field_in, jump_in, grad, kick, fgrad, sig_in, impulse, div, halves, face_at,
+    traces, jump, field_in, jump_in, grad, kick, fgrad, sig_in, impulse, div, halves, chosen_at,
     out_buf, in_buf, x_in, x_sum, z_out, z_in,
     load_sem, send_sem, recv_sem, x_send, x_recv, z_send, z_recv,
 ):
@@ -249,7 +249,9 @@
         for f in range(6):
             code = near[f : f + 1, :]
             own_tile[f], own_hit[f] = tile_of(code)
-            at = jnp.where(code >= slots + cap, code - (slots + cap - SIDE), code - slots)
+            side = jnp.where(code >= slots + cap, 1, 0)
+            at = code - slots - side * cap
+            at = at + jnp.right_shift(at, 8) * 256 + side * 256
             side_tile[f], side_hit[f] = tile_of(jnp.where(code >= slots, at, -1))
 
         def body(k, carry):
@@ -272,9 +274,11 @@
 
         lax.fori_loop(0, 2 * SIDE // 16, side_body, 0)
         ones = jnp.ones((16, slots), bf16)
-        face_at[...] = lax.dot_general(
+        face_at = lax.dot_general(
             ones, onehot[6], (((1,), (1,)), ((), ())), preferred_element_type=f32
         )
+        for f in range(6):
+            chosen_at[f] = jnp.where(face_at == f + 1.0, 1.0, 0.0).astype(bf16)
 
         def side_ones(k, carry):
             rows = pl.ds(pl.multiple_of(k * 16, 16), 16)
@@ -299,7 +303,7 @@
 
     pieces = [(side, piece) for piece in range(SIDE // 256) for side in range(2)]
 
-    def send(phase):
+    def send(phase, n):
         rows = traces[...].reshape(576, slots)
         for number, (side, piece) in enumerate(pieces):
             start = side * SIDE + piece * 256
@@ -310,6 +314,11 @@
                 both = got[f * 96 : f * 96 + 48] + got[f * 96 + 48 : f * 96 + 96]
                 total = jnp.where(face == f, both, total)
             out_buf[phase, side, piece] = total
+            if phase == 0 and number == 1:
+                @pl.when(n == 0)
+                def _():
+                    pl.semaphore_wait(barrier, 2 + len(peers))
+
             if number % 2:
                 for end in range(2):
                     copy_out(phase, end, piece).start()
@@ -322,29 +331,33 @@
             jump[f] = got[0:48] + got[48:96] - mine * weight
 
     def arrive(phase):
-        for side, piece in pieces:
-            copy_out(phase, side, piece).wait()
-        for side, piece in pieces:
-            start = side * SIDE + piece * 256
-            columns = slice(start, start + 256)
-            high, low = split(in_buf[phase, side, piece])
-            for f in range(6):
-                chosen = jnp.broadcast_to(
-                    jnp.where(face_at[0:1, columns] == f + 1.0, 1.0, 0.0), (16, 256)
-                ).astype(bf16)
-                for c in range(3):
-                    rows = slice(c * 16, c * 16 + 16)
-                    halves[f * 96 + c * 16 : f * 96 + c * 16 + 16, columns] = high[rows] * chosen
-                    halves[f * 96 + 48 + c * 16 : f * 96 + 64 + c * 16, columns] = low[rows] * chosen
-        for t in range(0, slots, 256):
-            columns = slice(t, t + 256)
-            got = dot(halves[...], onehot[6, :, columns])
-            for f in range(6):
-                total = jump[f, :, columns] + got[f * 96 : f * 96 + 48] + got[f * 96 + 48 : f * 96 + 96]
-                high, low = split(total)
-                for c in range(3):
-                    jump_in[c, f * 16 : f * 16 + 16, columns] = high[c * 16 : c * 16 + 16]
-                    jump_in[c, 96 + f * 16 : 112 + f * 16, columns] = low[c * 16 : c * 16 + 16]
+        last = SIDE // 256 - 1
+        for piece in range(last + 1):
+            for side in range(2):
+                copy_out(phase, side, piece).wait()
+            for side in range(2):
+                start = piece * 512 + side * 256
+                columns = slice(start, start + 256)
+                high, low = split(in_buf[phase, side, piece])
+                for f in range(6):
+                    chosen = chosen_at[f, :, columns]
+                    for c in range(3):
+                        rows = slice(c * 16, c * 16 + 16)
+                        halves[f * 96 + c * 16 : f * 96 + c * 16 + 16, columns] = high[rows] * chosen
+                        halves[f * 96 + 48 + c * 16 : f * 96 + 64 + c * 16, columns] = low[rows] * chosen
+            both = slice(piece * 512, piece * 512 + 512)
+            for t in range(0, slots, 256):
+                columns = slice(t, t + 256)
+                got = dot(halves[:, both], onehot[6, both, columns])
+                for f in range(6):
+                    total = jump[f, :, columns] + got[f * 96 : f * 96 + 48] + got[f * 96 + 48 : f * 96 + 96]
+                    if piece < last:
+                        jump[f, :, columns] = total
+                        continue
+                    high, low = split(total)
+                    for c in range(3):
+                        jump_in[c, f * 16 : f * 16 + 16, columns] = high[c * 16 : c * 16 + 16]
+                        jump_in[c, 96 + f * 16 : 112 + f * 16, columns] = low[c * 16 : c * 16 + 16]
 
     def put3(ref, index, high, low):
         ref[index, 0:64] = high
@@ -378,11 +391,7 @@
     def step(n, carry):
         velocity_traces()
 
-        @pl.when(n == 0)
-        def _():
-            pl.semaphore_wait(barrier, 2 + len(peers))
-
-        send(0)
+        send(0, n)
 
         @pl.when(n == 0)
         def _():
@@ -420,7 +429,7 @@
             for m, (i, j) in ((3, (0, 1)), (4, (0, 2)), (5, (1, 2))):
                 sig[m, rows, cols] = sig[m, rows, cols] + shear * (g[i][j] + g[j][i])
         stress_traces()
-        send(1)
+        send(1, n)
         for r, rows, cols in blocks:
             g = [[fgrad[i, j * 64 + r : j * 64 + r + 8, cols] for j in range(3)] for i in range(3)]
             s = [sig[m, rows, cols] for m in range(6)]
@@ -483,8 +492,10 @@
 
 
 def hand_out(vel_in, part_in, vel_out, part_out, vel, part, sem):
-    loads = [pltpu.make_async_copy(vel_in, vel, sem.at[0]), pltpu.make_async_copy(part_in, part, sem.at[1])]
-    stores = [pltpu.make_async_copy(vel, vel_out, sem.at[2]), pltpu.make_async_copy(part, part_out, sem.at[3])]
+    loads = [pltpu.make_async_copy(vel_in.at[0, c], vel.at[c], sem.at[0, c]) for c in range(3)]
+    loads.append(pltpu.make_async_copy(part_in, part, sem.at[0, 3]))
+    stores = [pltpu.make_async_copy(vel.at[c], vel_out.at[0, c], sem.at[1, c]) for c in range(3)]
+    stores.append(pltpu.make_async_copy(part, part_out, sem.at[1, 3]))
     for copy in loads:
         copy.start()
     for load, store in zip(loads, stores):
@@ -535,7 +546,7 @@
             pltpu.VMEM((3, 192, slots), f32),
             pltpu.VMEM((3, 64, slots), f32),
             pltpu.VMEM((576, 2 * SIDE), bf16),
-            pltpu.VMEM((16, 2 * SIDE), f32),
+            pltpu.VMEM((6, 16, 2 * SIDE), bf16),
             pltpu.VMEM((2, 2, SIDE // 256, 48, 256), f32),
             pltpu.VMEM((2, 2, SIDE // 256, 48, 256), f32),
             pltpu.VMEM((NX - 1, 3, 64 // NX, slots), f32),
@@ -565,9 +576,9 @@
         in_specs=[hbm, hbm],
         out_specs=(hbm, hbm),
         scratch_shapes=[
-            pltpu.VMEM(velocity.shape, f32),
+            pltpu.VMEM(velocity.shape[1:], f32),
             pltpu.VMEM(part.shape, f32),
-            pltpu.SemaphoreType.DMA((4,)),
+            pltpu.SemaphoreType.DMA((2, 4)),
         ],
     )(velocity, part)
 

time: 73.6 us -> 70.6 us (0.959)
  Pallas kernels: 72.8 us -> 69.7 us
    pallas_call x1, Pallas kernels: 70.9 us -> 67.9 us  [local(): pl.pallas_call(sim_kernel, out_shape=(jax.ShapeDtypeStruct((1, 3, 64, slo...]
where the time goes in v4:
time: 70.6 us; the launch traced here: 70.4 us
  Pallas kernels  69.7 us (99%)
    pallas_call x1, Pallas kernels, local(): pl.pallas_call(sim_kernel, out_shape=(jax.ShapeDtypeStruct((1, 3, 64, slo...  67.9 us
    pallas_call x1, Pallas kernels, local(): pl.pallas_call(hand_out, out_shape=tuple((jax.ShapeDtypeStruct(x.shape, f...  1.86 us

profile of v4, /device:TPU:25, one launch (start us, length us, event | category | flops | bytes accessed | tf_op | source)
XLA Modules:
  0.0 70.4 jit_solution(15050594209772068657)
XLA Ops:
  0.6 67.9 %shard_map.113 = (f32[1,3,64,768]{3,2,1,0:T(8,128)}, f32[3,1,1024]{2,1,0:T(1,128)}) custom-call(f32[1,9,64,768]{3,2,1,0:T(8,128)} %state.1, f32[1,3,3,64,768]{4,3,2,1,0:T(8,128)} %forward_hbm.1, f32[64,768]{1,0:T(8,128)} %rho.1, f32[64,768]{1,0:T(8,128)} %lam.1, f32[64,768]{1,0:T(8,128)} %mu.1, s32[6,768]{1,0:T(8,128)} %near.1, s32[2,440]{1,0:T(2,128)} %sends.1, ...), custom_call_target="tpu_custom_call" | custom-call | tf_op jit(solution)/shard_map/pallas_call | solution.py:517
  68.5 1.9 %shard_map.114 = (f32[1,3,64,768]{3,2,1,0:T(8,128)}, f32[3,1,1024]{2,1,0:T(1,128)}) custom-call(f32[1,3,64,768]{3,2,1,0:T(8,128)} %get-tuple-element.4.vel_in, f32[3,1,1024]{2,1,0:T(1,128)} %get-tuple-element.5.part_in), custom_call_target="tpu_custom_call" | custom-call | tf_op jit(solution)/shard_map/pallas_call | solution.py:573

commit v5 on v4

--- a/solution.py
+++ b/solution.py
@@ -14,6 +14,7 @@
 half_lift = 3.0
 symmetric_index = ((0, 3, 4), (3, 1, 5), (4, 5, 2))
 SIDE = 512
+PIECE = 128
 HALF = 384
 NX, NZ = 4, 12
 SUM_EVENTS = True
@@ -243,7 +244,7 @@
         pick[rows, :] = jnp.where(spread[0] == level, spread[1], jnp.zeros_like(level))
         return carry
 
-    lax.fori_loop(0, slots // 16, build_pick, 0)
+    lax.fori_loop(0, slots // 16, build_pick, 0, unroll=4)
 
     def build_onehot():
         for f in range(6):
@@ -251,7 +252,7 @@
             own_tile[f], own_hit[f] = tile_of(code)
             side = jnp.where(code >= slots + cap, 1, 0)
             at = code - slots - side * cap
-            at = at + jnp.right_shift(at, 8) * 256 + side * 256
+            at = at + jnp.right_shift(at, 7) * PIECE + side * PIECE
             side_tile[f], side_hit[f] = tile_of(jnp.where(code >= slots, at, -1))
 
         def body(k, carry):
@@ -261,7 +262,7 @@
                 onehot[f, rows, :] = jnp.where(own_tile[f] == level, own_hit[f], jnp.zeros_like(level))
             return carry
 
-        lax.fori_loop(0, slots // 16, body, 0)
+        lax.fori_loop(0, slots // 16, body, 0, unroll=2)
 
         def side_body(k, carry):
             rows = pl.ds(pl.multiple_of(k * 16, 16), 16)
@@ -272,7 +273,7 @@
             onehot[6, pl.ds(pl.multiple_of(k * 16, 16), 16), :] = total
             return carry
 
-        lax.fori_loop(0, 2 * SIDE // 16, side_body, 0)
+        lax.fori_loop(0, 2 * SIDE // 16, side_body, 0, unroll=2)
         ones = jnp.ones((16, slots), bf16)
         face_at = lax.dot_general(
             ones, onehot[6], (((1,), (1,)), ((), ())), preferred_element_type=f32
@@ -285,7 +286,7 @@
             onehot[6, rows, :] = jnp.minimum(onehot[6, rows, :], jnp.ones((16, slots), bf16))
             return carry
 
-        lax.fori_loop(0, 2 * SIDE // 16, side_ones, 0)
+        lax.fori_loop(0, 2 * SIDE // 16, side_ones, 0, unroll=4)
 
     def inner_of(f):
         return jnp.where(near[f : f + 1, :] >= 0, 1.0, 0.0)
@@ -313,15 +314,17 @@
             for f in range(6):
                 both = got[f * 96 : f * 96 + 48] + got[f * 96 + 48 : f * 96 + 96]
                 total = jnp.where(face == f, both, total)
-            out_buf[phase, side, piece] = total
+            for k in range(256 // PIECE):
+                out_buf[phase, side, piece * (256 // PIECE) + k] = total[:, k * PIECE : k * PIECE + PIECE]
             if phase == 0 and number == 1:
                 @pl.when(n == 0)
                 def _():
                     pl.semaphore_wait(barrier, 2 + len(peers))
 
             if number % 2:
-                for end in range(2):
-                    copy_out(phase, end, piece).start()
+                for k in range(256 // PIECE):
+                    for end in range(2):
+                        copy_out(phase, end, piece * (256 // PIECE) + k).start()
 
     def own(phase):
         for f in range(6):
@@ -331,13 +334,13 @@
             jump[f] = got[0:48] + got[48:96] - mine * weight
 
     def arrive(phase):
-        last = SIDE // 256 - 1
+        last = SIDE // PIECE - 1
         for piece in range(last + 1):
             for side in range(2):
                 copy_out(phase, side, piece).wait()
             for side in range(2):
-                start = piece * 512 + side * 256
-                columns = slice(start, start + 256)
+                start = (piece * 2 + side) * PIECE
+                columns = slice(start, start + PIECE)
                 high, low = split(in_buf[phase, side, piece])
                 for f in range(6):
                     chosen = chosen_at[f, :, columns]
@@ -345,7 +348,7 @@
                         rows = slice(c * 16, c * 16 + 16)
                         halves[f * 96 + c * 16 : f * 96 + c * 16 + 16, columns] = high[rows] * chosen
                         halves[f * 96 + 48 + c * 16 : f * 96 + 64 + c * 16, columns] = low[rows] * chosen
-            both = slice(piece * 512, piece * 512 + 512)
+            both = slice(piece * 2 * PIECE, piece * 2 * PIECE + 2 * PIECE)
             for t in range(0, slots, 256):
                 columns = slice(t, t + 256)
                 got = dot(halves[:, both], onehot[6, both, columns])
@@ -547,15 +550,15 @@
             pltpu.VMEM((3, 64, slots), f32),
             pltpu.VMEM((576, 2 * SIDE), bf16),
             pltpu.VMEM((6, 16, 2 * SIDE), bf16),
-            pltpu.VMEM((2, 2, SIDE // 256, 48, 256), f32),
-            pltpu.VMEM((2, 2, SIDE // 256, 48, 256), f32),
+            pltpu.VMEM((2, 2, SIDE // PIECE, 48, PIECE), f32),
+            pltpu.VMEM((2, 2, SIDE // PIECE, 48, PIECE), f32),
             pltpu.VMEM((NX - 1, 3, 64 // NX, slots), f32),
             pltpu.VMEM((3, 64 // NX, slots), f32),
             pltpu.VMEM((NZ, 3, share // 128, 128), f32),
             pltpu.VMEM((NZ - 1, 3, share // 128, 128), f32),
             pltpu.SemaphoreType.DMA((3,)),
-            pltpu.SemaphoreType.DMA((2, 2, SIDE // 256)),
-            pltpu.SemaphoreType.DMA((2, 2, SIDE // 256)),
+            pltpu.SemaphoreType.DMA((2, 2, SIDE // PIECE)),
+            pltpu.SemaphoreType.DMA((2, 2, SIDE // PIECE)),
             pltpu.SemaphoreType.DMA((2, NX - 1)),
             pltpu.SemaphoreType.DMA((2, NX - 1)),
             pltpu.SemaphoreType.DMA((2, NZ - 1)),

time: 70.6 us -> 69.2 us (0.980)
  Pallas kernels: 69.7 us -> 68.4 us
    pallas_call x1, Pallas kernels: 67.9 us -> 66.5 us  [local(): pl.pallas_call(sim_kernel, out_shape=(jax.ShapeDtypeStruct((1, 3, 64, slo...]
where the time goes in v5:
time: 69.2 us; the launch traced here: 69 us
  Pallas kernels  68.4 us (99%)
    pallas_call x1, Pallas kernels, local(): pl.pallas_call(sim_kernel, out_shape=(jax.ShapeDtypeStruct((1, 3, 64, slo...  66.5 us
    pallas_call x1, Pallas kernels, local(): pl.pallas_call(hand_out, out_shape=tuple((jax.ShapeDtypeStruct(x.shape, f...  1.86 us

profile of v5, /device:TPU:25, one launch (start us, length us, event | category | flops | bytes accessed | tf_op | source)
XLA Modules:
  0.0 69.0 jit_solution(11225301786078418802)
XLA Ops:
  0.6 66.5 %shard_map.113 = (f32[1,3,64,768]{3,2,1,0:T(8,128)}, f32[3,1,1024]{2,1,0:T(1,128)}) custom-call(f32[1,9,64,768]{3,2,1,0:T(8,128)} %state.1, f32[1,3,3,64,768]{4,3,2,1,0:T(8,128)} %forward_hbm.1, f32[64,768]{1,0:T(8,128)} %rho.1, f32[64,768]{1,0:T(8,128)} %lam.1, f32[64,768]{1,0:T(8,128)} %mu.1, s32[6,768]{1,0:T(8,128)} %near.1, s32[2,440]{1,0:T(2,128)} %sends.1, ...), custom_call_target="tpu_custom_call" | custom-call | tf_op jit(solution)/shard_map/pallas_call | solution.py:520
  67.2 1.9 %shard_map.114 = (f32[1,3,64,768]{3,2,1,0:T(8,128)}, f32[3,1,1024]{2,1,0:T(1,128)}) custom-call(f32[1,3,64,768]{3,2,1,0:T(8,128)} %get-tuple-element.4.vel_in, f32[3,1,1024]{2,1,0:T(1,128)} %get-tuple-element.5.part_in), custom_call_target="tpu_custom_call" | custom-call | tf_op jit(solution)/shard_map/pallas_call | solution.py:576
